TPU v7x, 256 devices: a whole 4x4x8 slice. The times are simulated.
256 devices in a mesh: row: 32 (over z, y), col: 8 (over x, core).
Axes of the slice: x: 4, y: 4, z: 8, core: 2. Of those that a mesh axis runs over, the one named last changes fastest.
Arguments:
- shot_dose: float32 [524288], P(('row', 'col')), may hold values from 0.25 to 4
- shot_owner: int32 [524288, 1], P(('row', 'col')), may hold values from 0 to 31; in each aligned block of 2048 rows (0 to 2047, 2048 to 4095, ...) at most 128 rows name the same one
- shot_cell: int32 [524288], P(('row', 'col')), may hold values from 0 to 15840
- shot_offset: int32 [524288], P(('row', 'col')), may hold values from 0 to 255
Outputs:
- final_dose: float32 [524288], P(('row', 'col'))
- backscatter_field: float32 [1024, 4096], P('row', 'col')
Inputs may be any that keep to these rules, and one draw needn't show every extreme that they name: `shot_owner`: among the 2048 shots of one device at most 128 name the same tile row, and some tile row is named by exactly that many. `shot_cell`: A cell cy * 511 + cx with cy below 31 and cx below 511. `shot_offset`: oy * 16 + ox.
All inputs are finite; a program needn't handle non-finite values.
Results may differ from a plain program's by a relative error of at most 0.0001.
Values sent between devices are 32-bit elements; how exact they have to be, the bound alone decides.
No kernel may reach another device: no remote copies, remote signals or barrier semaphores. Data moves between devices by JAX's collectives and lax.ppermute only.
A program may use at most 64 MiB of HBM per device.

v0:
```python
import jax
import jax.numpy as jnp
from jax import lax
from jax.sharding import PartitionSpec as P

CY = 32
CX = 512
HALF = 30
ITERS = 2


backscatter_ratio = 0.6
kernel_spread = 10.0


def extended(cells, sides, width):
    for axis, dim in sides:
        count = lax.axis_size(axis)
        ends = count - 1
        head = lax.slice_in_dim(cells, 0, width, axis=dim)
        tail = lax.slice_in_dim(cells, cells.shape[dim] - width, cells.shape[dim], axis=dim)
        cells = jnp.concatenate(
            [
                lax.ppermute(tail, axis, [(i, (i + 1) % count) for i in range(ends)]),
                cells,
                lax.ppermute(head, axis, [((i + 1) % count, i) for i in range(ends)]),
            ],
            axis=dim,
        )
    return cells


def tap_value(lags):
    inside = (lags >= 0) & (lags <= 2 * HALF)
    centered = (lags - HALF).astype(jnp.float32)
    all_lags = jnp.arange(2 * HALF + 1).astype(jnp.float32) - HALF
    normal = jnp.sum(jnp.exp(-(all_lags * all_lags) / (2.0 * kernel_spread * kernel_spread)))
    values = jnp.exp(-(centered * centered) / (2.0 * kernel_spread * kernel_spread)) / normal
    return jnp.where(inside, values, 0.0)


def matrix_left(length):
    rows_at = lax.broadcasted_iota(jnp.int32, (length, length + 2 * HALF), 0)
    cols_at = lax.broadcasted_iota(jnp.int32, (length, length + 2 * HALF), 1)
    return tap_value(cols_at - rows_at)


def matrix_right(length):
    rows_at = lax.broadcasted_iota(jnp.int32, (length + 2 * HALF, length), 0)
    cols_at = lax.broadcasted_iota(jnp.int32, (length + 2 * HALF, length), 1)
    return tap_value(rows_at - cols_at)


def blurred(density):
    left_taps = matrix_left(CY)
    right_taps = matrix_right(CX)
    highest = lax.Precision.HIGHEST
    padded = extended(density, (("row", 0),), HALF)
    along_y = jnp.dot(left_taps, padded, precision=highest, preferred_element_type=jnp.float32)
    widened = extended(along_y, (("col", 1),), HALF)
    return jnp.dot(widened, right_taps, precision=highest, preferred_element_type=jnp.float32)


def shot_geometry(cell_code, offset_code):
    cell_row = cell_code // (CX - 1)
    cell_col = cell_code % (CX - 1)
    base_cell = cell_row * CX + cell_col
    corners = jnp.stack([base_cell, base_cell + 1, base_cell + CX, base_cell + CX + 1])
    off_row = (offset_code // 16).astype(jnp.float32)
    off_col = (offset_code % 16).astype(jnp.float32)
    weights = (
        jnp.stack(
            [
                (16.0 - off_row) * (16.0 - off_col),
                (16.0 - off_row) * off_col,
                off_row * (16.0 - off_col),
                off_row * off_col,
            ]
        )
        / 256.0
    )
    return (corners, weights)


def slot_exposures(recv_corners, recv_weights, received):
    flat_density = (
        jnp.zeros((CY * CX,), jnp.float32)
        .at[recv_corners.reshape(-1)]
        .add((recv_weights * received[None, :]).reshape(-1))
    )
    density = flat_density.reshape(CY, CX)
    field_now = blurred(density)
    total_field = (density + backscatter_ratio * field_now).reshape(-1)
    return (jnp.sum(recv_weights * total_field[recv_corners], axis=0), field_now)


def per_device(shot_dose, shot_owner, shot_cell, shot_offset):
    n_rows = lax.axis_size("row")
    shot_count = shot_dose.shape[0]
    owners = shot_owner[:, 0]
    dose_now = shot_dose
    field_now = jnp.zeros((CY, CX), jnp.float32)
    capacity = 2 * shot_count // n_rows
    sorted_order = jnp.argsort(owners, stable=True)
    per_owner = jnp.sum(
        (owners[:, None] == jnp.arange(n_rows, dtype=jnp.int32)[None, :]).astype(jnp.int32), axis=0
    )
    owner_start = jnp.cumsum(per_owner) - per_owner
    sorted_owner = owners[sorted_order]
    sorted_rank = jnp.arange(shot_count, dtype=jnp.int32) - owner_start[sorted_owner]
    slot_rank = jnp.zeros((shot_count,), jnp.int32).at[sorted_order].set(sorted_rank)
    slot_index = owners * capacity + slot_rank
    packed = (
        jnp.zeros((n_rows * capacity,), jnp.int32).at[slot_index].set(shot_cell * 256 + shot_offset)
    )
    places = lax.all_to_all(
        packed.reshape(n_rows, capacity), "row", split_axis=0, concat_axis=0, tiled=True
    ).reshape(-1)
    recv_corners, recv_weights = shot_geometry(places // 256, places % 256)
    for iteration in range(ITERS):
        outgoing = jnp.zeros((n_rows * capacity,), jnp.float32).at[slot_index].set(dose_now)
        received = lax.all_to_all(
            outgoing.reshape(n_rows, capacity), "row", split_axis=0, concat_axis=0, tiled=True
        ).reshape(-1)
        slot_exposure, field_now = slot_exposures(recv_corners, recv_weights, received)
        returned = lax.all_to_all(
            slot_exposure.reshape(n_rows, capacity), "row", split_axis=0, concat_axis=0, tiled=True
        ).reshape(-1)
        exposure = returned[slot_index]
        dose_now = dose_now * (1.0 + backscatter_ratio) / exposure
    return (dose_now, field_now)


def solution(mesh):
    placed = (P(("row", "col")), P(("row", "col"), None), P(("row", "col")), P(("row", "col")))
    return jax.shard_map(
        per_device,
        mesh=mesh,
        in_specs=placed,
        out_specs=(P(("row", "col")), P("row", "col")),
        check_vma=False,
    )
```

profile of v0, /device:TPU:7, one launch (start us, length us, event | category | flops | bytes accessed | tf_op | source)
XLA Modules:
  0.0 604.7 jit_solution(17369539189939954403)
XLA Ops:
  0.6 0.9 convert_reduce_fusion
  1.7 0.1 reduce.1
  1.8 0.7 fusion.81
  2.5 0.7 fusion.80
  3.3 5.0 sort.17
  8.3 11.8 %gather_fusion = s32[2048]{0:T(1024)S(1)} fusion(s32[2048]{0:T(1024)S(1)} %bitcast.90, s32[2048]{0:T(1024)S(1)} %get-tuple-element.55), kind=kCustom, calls=%fused_computation | custom fusion | bytes 24576 | tf_op jit(solution)/shard_map/gather | solution.py:109
  20.1 4.4 compare_select_fusion.9
  24.5 0.6 compare_reduce_fusion.24
  25.1 15.7 %select_subtract_fusion = s32[2048]{0:T(1024)S(1)} fusion(pred[2048]{0:T(1024)(128)(4,1)S(1)} %get-tuple-element.28, pred[2048]{0:T(1024)(128)(4,1)S(1)} %get-tuple-element.27, pred[2048]{0:T(1024)(128)(4,1)S(1)} %get-tuple-element.26, pred[2048]{0:T(1024)(128)(4,1)S(1)} %get-tuple-element.25, pred[2048]{0:T(1024)(128)(4,1)S(1)} %get-tuple-element.24, ...), kind=kLoop, calls=%fused_computation.117 | loop fusion | flops 53248 | bytes 67684 | tf_op jit(solution)/shard_map/sub | solution.py:110
  40.9 8.0 %scatter_custom_fusion = s32[2048]{0:T(1024)S(1)} fusion(s32[2048]{0:T(1024)S(1)} %get-tuple-element.56, s32[2048]{0:T(1024)S(1)} %select_subtract_fusion, s32[]{:T(128)} %constant.94.clone.1), kind=kCustom, calls=%fused_computation.134 | custom fusion | bytes 8196 | tf_op jit(solution)/shard_map/scatter | solution.py:111
  49.0 8.6 %scatter_custom_fusion.1 = s32[4096]{0:T(1024)} fusion(s32[2048]{0:T(1024)S(1)} %get-tuple-element.30, s32[2048]{0:T(1024)S(1)} %get-tuple-element.89, s32[]{:T(128)} %constant.94.clone.1), kind=kCustom, calls=%fused_computation.129 | custom fusion | bytes 16388 | tf_op jit(solution)/shard_map/scatter | solution.py:114
  57.6 11.2 %all-to-all-start = ((s32[32,1,128]{2,1,0:T(1,128)}), s32[32,1,128]{2,1,0:T(1,128)S(1)}, u32[]{:S(2)}, u32[]{:S(2)}) async-start(s32[32,1,128]{2,1,0:T(1,128)} %bitcast.36), calls=%async_computation | async-start | bytes 32768 | tf_op jit(solution)/shard_map/all_to_all | solution.py:116
  68.8 8.6 %scatter_custom_fusion.2 = f32[4096]{0:T(1024)} fusion(s32[2048]{0:T(1024)S(1)} %get-tuple-element.30, f32[2048]{0:T(1024)S(1)} %copy-done.4, f32[]{:T(128)} %constant.107.clone.1), kind=kCustom, calls=%fused_computation.123 | custom fusion | bytes 16388 | tf_op jit(solution)/shard_map/scatter | solution.py:121
  77.4 0.6 exponential_reduce_fusion
  78.0 9.2 %all-to-all-start.1 = ((f32[32,1,128]{2,1,0:T(1,128)}), f32[32,1,128]{2,1,0:T(1,128)S(1)}, u32[]{:S(2)}, u32[]{:S(2)}) async-start(f32[32,1,128]{2,1,0:T(1,128)} %bitcast.39), calls=%async_computation.1 | async-start | bytes 32768 | tf_op jit(solution)/shard_map/all_to_all | solution.py:122
  87.3 0.2 fusion.71
  87.5 0.2 fusion.38
  87.7 8.1 %all-to-all-done.1 = f32[32,1,128]{2,1,0:T(1,128)S(1)} async-done(((f32[32,1,128]{2,1,0:T(1,128)}), f32[32,1,128]{2,1,0:T(1,128)S(1)}, u32[]{:S(2)}, u32[]{:S(2)}) %all-to-all-start.1) | async-done | bytes 16416 | tf_op jit(solution)/shard_map/all_to_all | solution.py:122
  96.2 85.8 %scatter_custom_fusion.3 = f32[16384]{0:T(1024)S(1)} fusion(s32[16384]{0:T(1024)S(1)} %bitcast.101, f32[16384]{0:T(1024)S(1)} %bitcast.103, f32[]{:T(128)} %constant.107.clone.1), kind=kCustom, calls=%fused_computation.69 | custom fusion | flops 16384 | bytes 65540 | tf_op jit(solution)/shard_map/scatter-add | solution.py:89
  182.1 21.1 %collective-permute-start = (f32[30,512]{1,0:T(8,128)S(1)}, f32[30,512]{1,0:T(8,128)S(1)}, u32[]{:S(2)}, u32[]{:S(2)}) collective-permute-start(f32[30,512]{1,0:T(8,128)S(1)} %slice.69), channel_id=1, source_target_pairs={{0,8},{8,16},{16,24},{24,32},{32,40},{40,48},{48,56},{56,64},{64,7... | collective-permute-start | bytes 184328 | tf_op jit(solution)/shard_map/ppermute | solution.py:24
  203.2 1.3 collective-permute-start.1
  204.7 3.6 collective-permute-done.1
  208.3 0.9 fusion.6
  209.2 1.3 collective-permute-start.2
  210.5 6.3 %collective-permute-start.3 = (f32[32,30]{1,0:T(8,128)S(1)}, f32[32,30]{1,0:T(8,128)S(1)}, u32[]{:S(2)}, u32[]{:S(2)}) collective-permute-start(f32[32,30]{1,0:T(8,128)S(1)} %get-tuple-element.44), channel_id=1, source_target_pairs={{1,0},{2,1},{3,2},{4,3},{5,4},{6,5},{7,6},{9,8},{10,9},{11,10},{12... | collective-permute-start | bytes 11528 | tf_op jit(solution)/shard_map/ppermute | solution.py:26
  216.9 0.8 collective-permute-done.3
  217.7 1.3 fusion.4
  219.0 90.5 %gather_fusion.1 = f32[16384]{0:T(1024)S(1)} fusion(f32[16384]{0:T(1024)S(1)} %bitcast.87, s32[16384]{0:T(1024)S(1)} %broadcast_clamp_fusion), kind=kCustom, calls=%fused_computation.1 | custom fusion | bytes 196608 | tf_op jit(solution)/shard_map/gather | solution.py:94
  309.6 0.1 multiply_reduce_fusion.1
  309.7 17.3 %all_to_all.45 = f32[32,1,128]{2,1,0:T(1,128)S(1)} all-to-all(f32[32,1,128]{2,1,0:T(1,128)S(1)} %bitcast.99), channel_id=1, replica_groups=mesh['row'=32,'col'=8] {'row'}, dimensions={0} | all-to-all | bytes 32768 | tf_op jit(solution)/shard_map/all_to_all | solution.py:126
  327.0 11.8 %gather_fusion.2 = f32[2048]{0:T(1024)S(1)} fusion(f32[4096]{0:T(1024)S(1)} %bitcast.92, s32[2048]{0:T(1024)S(1)} %get-tuple-element.29), kind=kCustom, calls=%fused_computation.2 | custom fusion | bytes 24576 | tf_op jit(solution)/shard_map/gather | solution.py:129
  338.8 8.2 %scatter_custom_fusion.4 = f32[4096]{0:T(1024)S(1)} fusion(s32[2048]{0:T(1024)S(1)} %get-tuple-element.30, f32[2048]{0:T(1024)S(1)} %multiply_divide_fusion.1, f32[]{:T(128)} %constant.107.clone.1), kind=kCustom, calls=%fused_computation.121 | custom fusion | bytes 16388 | tf_op jit(solution)/shard_map/scatter | solution.py:121
  347.0 11.6 %all_to_all.46 = f32[32,1,128]{2,1,0:T(1,128)S(1)} all-to-all(f32[32,1,128]{2,1,0:T(1,128)S(1)} %bitcast.105), channel_id=1, replica_groups=mesh['row'=32,'col'=8] {'row'}, dimensions={0} | all-to-all | bytes 32768 | tf_op jit(solution)/shard_map/all_to_all | solution.py:122
  358.7 85.8 %scatter_custom_fusion.5 = f32[16384]{0:T(1024)S(1)} fusion(s32[16384]{0:T(1024)S(1)} %bitcast.102, f32[16384]{0:T(1024)S(1)} %bitcast.104, f32[]{:T(128)} %constant.107.clone.1), kind=kCustom, calls=%fused_computation.67 | custom fusion | flops 16384 | bytes 65540 | tf_op jit(solution)/shard_map/scatter-add | solution.py:89
  444.6 21.1 %collective-permute-start.4 = (f32[30,512]{1,0:T(8,128)S(1)}, f32[30,512]{1,0:T(8,128)S(1)}, u32[]{:S(2)}, u32[]{:S(2)}) collective-permute-start(f32[30,512]{1,0:T(8,128)S(1)} %slice.75), channel_id=1, source_target_pairs={{0,8},{8,16},{16,24},{24,32},{32,40},{40,48},{48,56},{56,64},{64,7... | collective-permute-start | bytes 184328 | tf_op jit(solution)/shard_map/ppermute | solution.py:24
  465.7 1.3 collective-permute-start.5
  467.0 3.7 collective-permute-done.5
  470.7 0.9 fusion.12
  471.7 1.3 collective-permute-start.6
  473.0 8.6 %collective-permute-start.7 = (f32[32,30]{1,0:T(8,128)S(1)}, f32[32,30]{1,0:T(8,128)S(1)}, u32[]{:S(2)}, u32[]{:S(2)}) collective-permute-start(f32[32,30]{1,0:T(8,128)S(1)} %get-tuple-element.40), channel_id=1, source_target_pairs={{1,0},{2,1},{3,2},{4,3},{5,4},{6,5},{7,6},{9,8},{10,9},{11,10},{12... | collective-permute-start | bytes 11528 | tf_op jit(solution)/shard_map/ppermute | solution.py:26
  481.6 0.8 collective-permute-done.7
  482.4 1.3 fusion.5
  483.7 0.6 copy-done.1
  484.3 90.5 %gather_fusion.3 = f32[16384]{0:T(1024)S(1)} fusion(f32[16384]{0:T(1024)S(1)} %bitcast.86, s32[16384]{0:T(1024)S(1)} %broadcast_clamp_fusion), kind=kCustom, calls=%fused_computation.3 | custom fusion | bytes 196608 | tf_op jit(solution)/shard_map/gather | solution.py:94
  574.9 0.1 multiply_reduce_fusion
  575.0 17.3 %all_to_all.47 = f32[32,1,128]{2,1,0:T(1,128)S(1)} all-to-all(f32[32,1,128]{2,1,0:T(1,128)S(1)} %bitcast.97), channel_id=1, replica_groups=mesh['row'=32,'col'=8] {'row'}, dimensions={0} | all-to-all | bytes 32768 | tf_op jit(solution)/shard_map/all_to_all | solution.py:126
  592.3 11.8 %gather_fusion.4 = f32[2048]{0:T(1024)S(1)} fusion(f32[4096]{0:T(1024)S(1)} %bitcast.93, s32[2048]{0:T(1024)S(1)} %get-tuple-element.29), kind=kCustom, calls=%fused_computation.4 | custom fusion | bytes 24576 | tf_op jit(solution)/shard_map/gather | solution.py:129
  604.1 0.6 multiply_divide_fusion
  (49 shorter events, 1.1 us)
Async XLA Ops:
  0.6 2.6 copy-start
  25.1 23.8 %copy-start.2 = (s32[2048]{0:T(1024)S(1)}, s32[2048]{0:T(1024)}, u32[]{:S(2)}) copy-start(s32[2048]{0:T(1024)} %param.7) | copy-start | bytes 24580
  25.1 23.8 %copy-start.3 = (s32[2048]{0:T(1024)S(1)}, s32[2048]{0:T(1024)}, u32[]{:S(2)}) copy-start(s32[2048]{0:T(1024)} %param.6) | copy-start | bytes 24580
  40.8 27.9 %copy-start.4 = (f32[2048]{0:T(1024)S(1)}, f32[2048]{0:T(1024)}, u32[]{:S(2)}) copy-start(f32[2048]{0:T(1024)} %param.4) | copy-start | bytes 24580
  57.6 20.5 %all-to-all-start = ((s32[32,1,128]{2,1,0:T(1,128)}), s32[32,1,128]{2,1,0:T(1,128)S(1)}, u32[]{:S(2)}, u32[]{:S(2)}) async-start(s32[32,1,128]{2,1,0:T(1,128)} %bitcast.36), calls=%async_computation | async-start | bytes 32768 | tf_op jit(solution)/shard_map/all_to_all | solution.py:116
  78.0 17.8 %all-to-all-start.1 = ((f32[32,1,128]{2,1,0:T(1,128)}), f32[32,1,128]{2,1,0:T(1,128)S(1)}, u32[]{:S(2)}, u32[]{:S(2)}) async-start(f32[32,1,128]{2,1,0:T(1,128)} %bitcast.39), calls=%async_computation.1 | async-start | bytes 32768 | tf_op jit(solution)/shard_map/all_to_all | solution.py:122
  182.1 22.5 %collective-permute-start = (f32[30,512]{1,0:T(8,128)S(1)}, f32[30,512]{1,0:T(8,128)S(1)}, u32[]{:S(2)}, u32[]{:S(2)}) collective-permute-start(f32[30,512]{1,0:T(8,128)S(1)} %slice.69), channel_id=1, source_target_pairs={{0,8},{8,16},{16,24},{24,32},{32,40},{40,48},{48,56},{56,64},{64,7... | collective-permute-start | bytes 184328 | tf_op jit(solution)/shard_map/ppermute | solution.py:24
  203.2 5.0 collective-permute-start.1
  209.2 7.6 %collective-permute-start.2 = (f32[32,30]{1,0:T(8,128)S(1)}, f32[32,30]{1,0:T(8,128)S(1)}, u32[]{:S(2)}, u32[]{:S(2)}) collective-permute-start(f32[32,30]{1,0:T(8,128)S(1)} %get-tuple-element.43), channel_id=1, source_target_pairs={{0,1},{1,2},{2,3},{3,4},{4,5},{5,6},{6,7},{8,9},{9,10},{10,11},{11... | collective-permute-start | bytes 11528 | tf_op jit(solution)/shard_map/ppermute | solution.py:24
  210.5 7.1 %collective-permute-start.3 = (f32[32,30]{1,0:T(8,128)S(1)}, f32[32,30]{1,0:T(8,128)S(1)}, u32[]{:S(2)}, u32[]{:S(2)}) collective-permute-start(f32[32,30]{1,0:T(8,128)S(1)} %get-tuple-element.44), channel_id=1, source_target_pairs={{1,0},{2,1},{3,2},{4,3},{5,4},{6,5},{7,6},{9,8},{10,9},{11,10},{12... | collective-permute-start | bytes 11528 | tf_op jit(solution)/shard_map/ppermute | solution.py:26
  444.6 22.4 %collective-permute-start.4 = (f32[30,512]{1,0:T(8,128)S(1)}, f32[30,512]{1,0:T(8,128)S(1)}, u32[]{:S(2)}, u32[]{:S(2)}) collective-permute-start(f32[30,512]{1,0:T(8,128)S(1)} %slice.75), channel_id=1, source_target_pairs={{0,8},{8,16},{16,24},{24,32},{32,40},{40,48},{48,56},{56,64},{64,7... | collective-permute-start | bytes 184328 | tf_op jit(solution)/shard_map/ppermute | solution.py:24
  465.7 5.0 collective-permute-start.5
  471.7 9.9 %collective-permute-start.6 = (f32[32,30]{1,0:T(8,128)S(1)}, f32[32,30]{1,0:T(8,128)S(1)}, u32[]{:S(2)}, u32[]{:S(2)}) collective-permute-start(f32[32,30]{1,0:T(8,128)S(1)} %get-tuple-element.39), channel_id=1, source_target_pairs={{0,1},{1,2},{2,3},{3,4},{4,5},{5,6},{6,7},{8,9},{9,10},{10,11},{11... | collective-permute-start | bytes 11528 | tf_op jit(solution)/shard_map/ppermute | solution.py:24
  473.0 9.4 %collective-permute-start.7 = (f32[32,30]{1,0:T(8,128)S(1)}, f32[32,30]{1,0:T(8,128)S(1)}, u32[]{:S(2)}, u32[]{:S(2)}) collective-permute-start(f32[32,30]{1,0:T(8,128)S(1)} %get-tuple-element.40), channel_id=1, source_target_pairs={{1,0},{2,1},{3,2},{4,3},{5,4},{6,5},{7,6},{9,8},{10,9},{11,10},{12... | collective-permute-start | bytes 11528 | tf_op jit(solution)/shard_map/ppermute | solution.py:26
  483.7 0.6 copy-start.1
where the time goes:
time: 609 us; the launch traced here: 605 us
  local copies, waits for them, and re-layouts  252 us (41%)
  other arithmetic  201 us (33%)
  starting transfers between devices  82.6 us (14%)
  blocking collectives  46.1 us (8%)
  waiting for transfers between devices  17 us (3%)
    gather x4, local copies, waits for them, and re-layouts, slot_exposures(): total_field[recv_corners]  181 us
    scatter-add x2, other arithmetic, slot_exposures(): flat_density = jnp.zeros((CY * CX,), jnp.float32).at[recv_corners.reshape...  172 us
    ppermute x4, starting transfers between devices, extended(): lax.ppermute(tail, axis, [(i, (i + 1) % count) for i in range(ends)])  44.7 us
    all_to_all x2, blocking collectives, per_device(): lax.all_to_all(slot_exposure.reshape(n_rows, capacity), 'row', split_axis...  34.5 us
    gather x2, local copies, waits for them, and re-layouts, per_device(): exposure = returned[slot_index]  23.5 us
    ppermute x4, starting transfers between devices, extended(): lax.ppermute(head, axis, [((i + 1) % count, i) for i in range(ends)])  17.5 us
    scatter x2, local copies, waits for them, and re-layouts, per_device(): jnp.zeros((n_rows * capacity,), jnp.float32).at[slot_index].set(dose_now)  16.9 us
    sub x1, other arithmetic, per_device(): jnp.arange(shot_count, dtype=jnp.int32) - owner_start[sorted_owner]  15.7 us
  transfers between devices with their start and end apart: 10, of which 5 were waited for; matrix products, arithmetic and copies ran while one was open for 2% of the time, Pallas kernels for 0%

commit v1 on v0

v1 whole, which is shorter than its diff:
```python
import jax
import jax.numpy as jnp
import numpy as np
from jax import lax
from jax.experimental import pallas as pl
from jax.experimental.pallas import tpu as pltpu
from jax.sharding import PartitionSpec as P

CY = 32
CX = 512
HALF = 30
N_ROW = 32
N_COL = 8
S_DEV = 2048
CAP = 128
REACH = 2
NT = 2 * REACH + 1
BLK = 128
NB = CX // BLK
XR = BLK + 16
SLOTS = N_ROW * CAP
BF = jnp.bfloat16
F32 = jnp.float32

BACKSCATTER = 0.6
SPREAD = 10.0


def taps():
    lags = np.arange(2 * HALF + 1, dtype=np.float64) - HALF
    values = np.exp(-(lags * lags) / (2.0 * SPREAD * SPREAD))
    return values / values.sum()


def band(rows, cols, offset):
    lag = np.arange(cols)[None, :] - np.arange(rows)[:, None] - offset + HALF
    t = taps()
    return np.where((lag >= 0) & (lag <= 2 * HALF), t[np.clip(lag, 0, 2 * HALF)], 0.0)


def two(m):
    hi = m.astype(jnp.bfloat16)
    lo = (m - hi.astype(np.float64)).astype(jnp.bfloat16)
    return np.asarray(hi), np.asarray(lo)


def left_constant(rows, cols, offset):
    hi, lo = two(band(rows, cols, offset))
    return np.concatenate([np.concatenate([hi, hi], 1), np.concatenate([lo, lo], 1)], 0)


def right_constant():
    hi, lo = two(band(BLK, 3 * BLK, BLK).T)
    return np.concatenate([hi, lo], 1)


def split2(v):
    hi = v.astype(BF)
    lo = (v - hi.astype(F32)).astype(BF)
    return hi, lo


def split3(v):
    hi = v.astype(BF).astype(F32)
    rest = v - hi
    mid = rest.astype(BF).astype(F32)
    return hi, mid, rest - mid


def nt_dot(a, b):
    return lax.dot_general(a, b, (((1,), (1,)), ((), ())), preferred_element_type=F32)


def nn_dot(a, b):
    return lax.dot_general(a, b, (((1,), (0,)), ((), ())), preferred_element_type=F32)


def shifted_rows(v, by):
    if by == 0:
        return v
    pad = jnp.zeros((abs(by), v.shape[1]), v.dtype)
    return jnp.concatenate([v[by:], pad], 0) if by > 0 else jnp.concatenate([pad, v[:by]], 0)


def pack_kernel(dose_ref, owner_ref, cell_ref, offset_ref, send_ref, rank_ref):
    owner = owner_ref[...]
    place = (cell_ref[...] * 256 + offset_ref[...]).astype(F32)
    dose = dose_ref[...]
    chunk = 256
    n_chunks = S_DEV // chunk
    mine = owner == lax.broadcasted_iota(jnp.int32, (N_ROW, S_DEV), 0)
    ones = jnp.where(mine, 1.0, 0.0)
    stacked = jnp.concatenate([ones[:, c * chunk:(c + 1) * chunk] for c in range(n_chunks)], 0).astype(BF)
    rows_at = lax.broadcasted_iota(jnp.int32, (chunk, chunk), 0)
    cols_at = lax.broadcasted_iota(jnp.int32, (chunk, chunk), 1)
    before = jnp.where(rows_at < cols_at, 1.0, 0.0).astype(BF)
    prefix = nn_dot(stacked, before)
    totals = nn_dot(stacked, jnp.ones((chunk, chunk), BF))
    base = jnp.zeros((N_ROW, chunk), F32)
    ranks = []
    for c in range(n_chunks):
        here = slice(c * N_ROW, (c + 1) * N_ROW)
        inside = ones[:, c * chunk:(c + 1) * chunk]
        ranks.append(jnp.sum(inside * (prefix[here] + base), axis=0, keepdims=True))
        base = base + totals[here]
    rank = jnp.concatenate(ranks, 1)
    rank_ref[...] = rank
    at_rank = jnp.where(rank == lax.broadcasted_iota(jnp.int32, (CAP, S_DEV), 0).astype(F32), 1.0, 0.0).astype(BF)
    parts = [jnp.where(mine, part, 0.0).astype(BF) for part in split3(place) + split3(dose)]
    packed = nt_dot(jnp.concatenate(parts, 0), at_rank)
    for which in range(2):
        p = packed[3 * which * N_ROW:3 * (which + 1) * N_ROW]
        whole = p[:N_ROW] + p[N_ROW:2 * N_ROW] + p[2 * N_ROW:]
        for t in range(NT):
            start = (2 * t + which) * CAP
            send_ref[:, 0, start:start + CAP] = shifted_rows(whole, t - REACH)


def decoded(place):
    cell = jnp.floor(place * (1.0 / 256.0))
    fine = place - 256.0 * cell
    cell_y = jnp.floor((cell + 0.5) * (1.0 / (CX - 1)))
    cell_x = cell - (CX - 1) * cell_y
    off_y = jnp.floor(fine * (1.0 / 16.0))
    off_x = fine - 16.0 * off_y
    block = jnp.floor(cell_x * (1.0 / BLK))
    return block, cell_y, cell_x - BLK * block, off_y * (1.0 / 16.0), off_x * (1.0 / 16.0)


def over_rows(v, rows):
    return jnp.broadcast_to(v, (rows, v.shape[1])).astype(BF)


def build_columns(column, off_x, b_ref, rows0):
    for i in range(N_ROW):
        here = slice(i * CAP, (i + 1) * CAP)
        at = lax.broadcasted_iota(jnp.int32, (XR, CAP), 0).astype(F32).astype(BF)
        first = over_rows(column[i:i + 1], XR)
        second = over_rows(column[i:i + 1] + 1.0, XR)
        w0 = over_rows(1.0 - off_x[i:i + 1], XR)
        w1 = over_rows(off_x[i:i + 1], XR)
        b_ref[rows0:rows0 + XR, here] = jnp.where(at == first, w0, jnp.where(at == second, w1, jnp.zeros_like(w0)))


def build_rows(key, off_y, dose, a_ref):
    hi0, lo0 = split2((1.0 - off_y) * dose)
    hi1, lo1 = split2(off_y * dose)
    hi0, lo0, hi1, lo1 = (v.astype(F32) for v in (hi0, lo0, hi1, lo1))
    for i in range(N_ROW):
        here = slice(i * CAP, (i + 1) * CAP)
        at = lax.broadcasted_iota(jnp.int32, (BLK, CAP), 0).astype(F32).astype(BF)
        first = at == over_rows(key[i:i + 1], BLK)
        second = at == over_rows(key[i:i + 1] + 1.0, BLK)
        for part, (p0, p1) in enumerate(((hi0, hi1), (lo0, lo1))):
            q0, q1 = over_rows(p0[i:i + 1], BLK), over_rows(p1[i:i + 1], BLK)
            a_ref[part * BLK:(part + 1) * BLK, here] = jnp.where(first, q0, jnp.where(second, q1, jnp.zeros_like(q0)))


def tile_density(a, b):
    both = nt_dot(a, b)
    d = both[:BLK] + both[BLK:]
    blocks = [d[:CY, :BLK]]
    for h in range(1, NB):
        over = d[(h - 1) * CY:h * CY, BLK:XR]
        over = jnp.concatenate([over, jnp.zeros((CY, BLK - XR + BLK), F32)], 1)
        blocks.append(d[h * CY:(h + 1) * CY, :BLK] + over)
    return jnp.concatenate(blocks, 1)


def packed_edge(block, lane0):
    rows = block.shape[0] // 4
    lane = lax.broadcasted_iota(jnp.int32, (rows, BLK), 1)
    out = jnp.zeros((rows, BLK), block.dtype)
    for g in range(4):
        part = block[g * rows:(g + 1) * rows]
        shift = (32 * g - lane0) % BLK
        part = pltpu.roll(part, shift, 1) if shift else part
        out = jnp.where(lane // 32 == g, part, out)
    return out


def unpacked_edge(edge, lane0):
    parts = []
    for g in range(4):
        shift = (lane0 - 32 * g) % BLK
        parts.append(pltpu.roll(edge, shift, 1) if shift else edge)
    return jnp.concatenate(parts, 0)


def blurred_y(density, taps_ref):
    hi, lo = split2(density)
    both = nn_dot(taps_ref[...], jnp.concatenate([hi, lo], 0))
    rows = both.shape[0] // 2
    return both[:rows] + both[rows:]


def blurred_x(along_y, left, right, taps_ref):
    wide = jnp.concatenate([left, along_y, right], 1)
    rows = along_y.shape[0]
    stacked = jnp.concatenate([wide[:, h * BLK:(h + 3) * BLK] for h in range(NB)], 0)
    hi, lo = split2(stacked)
    both = nn_dot(jnp.concatenate([hi, lo], 0), taps_ref[...])
    both = both[:NB * rows] + both[NB * rows:]
    out = both[:, :BLK] + both[:, BLK:]
    return jnp.concatenate([out[h * rows:(h + 1) * rows] for h in range(NB)], 1)


def gathered(total, key_block, cell_y, off_y, b):
    pieces = []
    for h in range(NB):
        inside = total[:, h * BLK:(h + 1) * BLK]
        if h + 1 < NB:
            after = total[:, (h + 1) * BLK:(h + 1) * BLK + XR - BLK]
        else:
            after = jnp.zeros((CY, XR - BLK), F32)
        pieces.append(jnp.concatenate([inside, after], 1))
    hi, lo = split2(jnp.concatenate(pieces, 0))
    both = nn_dot(jnp.concatenate([hi, lo], 0), b)
    at = lax.broadcasted_iota(jnp.int32, (CY, CAP), 0).astype(F32)
    rows = []
    for i in range(N_ROW):
        here = slice(i * CAP, (i + 1) * CAP)
        g = both[:BLK, here] + both[BLK:, here]
        block = key_block[i:i + 1]
        mine = g[:CY]
        for h in range(1, NB):
            mine = jnp.where(block == float(h), g[h * CY:(h + 1) * CY], mine)
        y, o = cell_y[i:i + 1], off_y[i:i + 1]
        w = jnp.where(at == y, 1.0 - o, jnp.where(at == y + 1.0, o, 0.0))
        rows.append(jnp.sum(w * mine, axis=0, keepdims=True))
    return jnp.concatenate(rows, 0)


def corrected(dose, exposure):
    return jnp.where(dose > 0.0, dose * (1.0 + BACKSCATTER) / exposure, 0.0)


def first_kernel(recv_ref, ltaps_ref, along_ref, density_ref, to_left_ref, to_right_ref, a_ref, b_ref):
    tiles = []
    for t in range(NT):
        place = recv_ref[:, 0, 2 * t * CAP:(2 * t + 1) * CAP]
        dose = recv_ref[:, 0, (2 * t + 1) * CAP:(2 * t + 2) * CAP]
        block, cell_y, column, off_y, off_x = decoded(place)
        build_columns(column, off_x, b_ref, 0)
        build_rows(block * CY + cell_y, off_y, dose, a_ref)
        tiles.append(tile_density(a_ref[...], b_ref[...]))
    density_ref[...] = jnp.concatenate(tiles[1:NT - 1], 0)
    along = blurred_y(jnp.concatenate(tiles, 0), ltaps_ref)
    along_ref[...] = along
    to_left_ref[...] = packed_edge(along[:, :BLK], 0)
    to_right_ref[...] = packed_edge(along[:, CX - BLK:], BLK - 32)


def second_kernel(sides_ref, recv_ref, along_ref, density_ref, from_left_ref, from_right_ref, rtaps_ref, ltaps_ref,
                  dose_ref, along2_ref, density2_ref, to_left_ref, to_right_ref, a_ref, b_ref):
    left = unpacked_edge(from_left_ref[...] * sides_ref[0], BLK - 32)
    right = unpacked_edge(from_right_ref[...] * sides_ref[1], 0)
    field = blurred_x(along_ref[...], left, right, rtaps_ref)
    total = density_ref[...] + BACKSCATTER * field
    tiles = []
    for n in range(NT - 2):
        t = n + 1
        place = recv_ref[:, 0, 2 * t * CAP:(2 * t + 1) * CAP]
        dose = recv_ref[:, 0, (2 * t + 1) * CAP:(2 * t + 2) * CAP]
        block, cell_y, column, off_y, off_x = decoded(place)
        build_columns(column, off_x, b_ref, 0)
        exposure = gathered(total[n * CY:(n + 1) * CY], block, cell_y, off_y, b_ref[...])
        dose = corrected(dose, exposure)
        if t == REACH:
            dose_ref[...] = dose
        build_rows(block * CY + cell_y, off_y, dose, a_ref)
        tiles.append(tile_density(a_ref[...], b_ref[...]))
    density2_ref[...] = tiles[1]
    along = blurred_y(jnp.concatenate(tiles, 0), ltaps_ref)
    along2_ref[...] = along
    to_left_ref[...] = packed_edge(along[:, :BLK], 0)
    to_right_ref[...] = packed_edge(along[:, CX - BLK:], BLK - 32)


def third_kernel(sides_ref, recv_ref, dose_ref, along_ref, density_ref, from_left_ref, from_right_ref, rtaps_ref,
                 field_ref, final_ref, b_ref):
    left = unpacked_edge(from_left_ref[...] * sides_ref[0], BLK - 32)
    right = unpacked_edge(from_right_ref[...] * sides_ref[1], 0)
    field = blurred_x(along_ref[...], left, right, rtaps_ref)
    field_ref[...] = field
    total = density_ref[...] + BACKSCATTER * field
    place = recv_ref[:, 0, 2 * REACH * CAP:(2 * REACH + 1) * CAP]
    block, cell_y, column, off_y, off_x = decoded(place)
    build_columns(column, off_x, b_ref, 0)
    exposure = gathered(total, block, cell_y, off_y, b_ref[...])
    final_ref[:, 0, :] = corrected(dose_ref[...], exposure)


def unpack_kernel(ret_ref, owner_ref, rank_ref, out_ref):
    mine = owner_ref[...] == lax.broadcasted_iota(jnp.int32, (N_ROW, S_DEV), 0)
    at_rank = jnp.where(rank_ref[...] == lax.broadcasted_iota(jnp.int32, (CAP, S_DEV), 0).astype(F32), 1.0, 0.0).astype(BF)
    parts = jnp.concatenate([p.astype(BF) for p in split3(ret_ref[:, 0, :])], 0)
    g = nn_dot(parts, at_rank)
    whole = g[:N_ROW] + g[N_ROW:2 * N_ROW] + g[2 * N_ROW:]
    out_ref[...] = jnp.sum(jnp.where(mine, whole, 0.0), axis=0, keepdims=True)


def vmem():
    return pl.BlockSpec(memory_space=pltpu.VMEM)


def call(kernel, outs, n_in, scratch=(), scalars=0):
    return pl.pallas_call(
        kernel,
        out_shape=[jax.ShapeDtypeStruct(s, F32) for s in outs],
        in_specs=[pl.BlockSpec(memory_space=pltpu.SMEM)] * scalars + [vmem()] * (n_in - scalars),
        out_specs=[vmem() for _ in outs],
        scratch_shapes=list(scratch),
        compiler_params=pltpu.CompilerParams(vmem_limit_bytes=48 << 20),
    )


def exchanged(to_left, to_right):
    n = lax.axis_size("col")
    from_left = lax.ppermute(to_right, "col", [(i, (i + 1) % n) for i in range(n)])
    from_right = lax.ppermute(to_left, "col", [((i + 1) % n, i) for i in range(n)])
    return from_left, from_right


def per_device(shot_dose, shot_owner, shot_cell, shot_offset):
    col = lax.axis_index("col")
    sides = jnp.stack([col > 0, col < N_COL - 1]).astype(F32)
    owner = shot_owner.reshape(1, S_DEV)
    ltaps = jnp.asarray(left_constant(3 * CY, NT * CY, CY))
    ltaps2 = jnp.asarray(left_constant(CY, 3 * CY, CY))
    rtaps = jnp.asarray(right_constant())
    send, rank = call(pack_kernel, [(N_ROW, 1, 2 * NT * CAP), (1, S_DEV)], 4)(
        shot_dose.reshape(1, S_DEV), owner, shot_cell.reshape(1, S_DEV), shot_offset.reshape(1, S_DEV)
    )
    recv = lax.all_to_all(send, "row", split_axis=0, concat_axis=0, tiled=True)
    a_scratch, b_scratch = pltpu.VMEM((2 * BLK, SLOTS), BF), pltpu.VMEM((XR, SLOTS), BF)
    edge = (3 * CY // 4, BLK)
    along, density, to_left, to_right = call(
        first_kernel, [(3 * CY, CX), (3 * CY, CX), edge, edge], 2, (a_scratch, b_scratch)
    )(recv, ltaps)
    from_left, from_right = exchanged(to_left, to_right)
    edge = (CY // 4, BLK)
    dose, along, density, to_left, to_right = call(
        second_kernel, [(N_ROW, CAP), (CY, CX), (CY, CX), edge, edge], 8, (a_scratch, b_scratch), 1
    )(sides, recv, along, density, from_left, from_right, rtaps, ltaps2)
    from_left, from_right = exchanged(to_left, to_right)
    field, final = call(third_kernel, [(CY, CX), (N_ROW, 1, CAP)], 8, (b_scratch,), 1)(
        sides, recv, dose, along, density, from_left, from_right, rtaps
    )
    back = lax.all_to_all(final, "row", split_axis=0, concat_axis=0, tiled=True)
    (out,) = call(unpack_kernel, [(1, S_DEV)], 3)(back, owner, rank)
    return out.reshape(S_DEV), field


def solution(mesh):
    placed = (P(("row", "col")), P(("row", "col"), None), P(("row", "col")), P(("row", "col")))
    return jax.shard_map(
        per_device,
        mesh=mesh,
        in_specs=placed,
        out_specs=(P(("row", "col")), P("row", "col")),
        check_vma=False,
    )
```

time: 609 us -> 65.7 us (0.11)
  local copies, waits for them, and re-layouts: 252 us -> 2.8 us
  other arithmetic: 201 us -> 0.08 us
  starting transfers between devices: 82.6 us -> 14.4 us
  blocking collectives: 46.1 us -> 11.7 us
  Pallas kernels: 0 us -> 18 us
    gather x9 -> x0, local copies, waits for them, and re-layouts: 218 us -> none  [the longest x4 181 us: slot_exposures(): total_field[recv_corners]]
    scatter-add x2 -> x0, other arithmetic: 172 us -> none  [slot_exposures(): flat_density = jnp.zeros((CY * CX,), jnp.float32).at[recv_corners.reshape...]
    ppermute x8 -> x4, starting transfers between devices: 62.2 us -> 3.07 us  [the longest x2 2.59 us: exchanged(): lax.ppermute(to_right, 'col', [(i, (i + 1) % n) for i in range(n)])]
    all_to_all x3 -> x1, blocking collectives: 46.1 us -> 11.7 us  [per_device(): back = lax.all_to_all(final, 'row', split_axis=0, concat_axis=0, tiled=True)]
    scatter x4 -> x0, local copies, waits for them, and re-layouts: 33.5 us -> none  [the longest x2 16.9 us: per_device(): jnp.zeros((n_rows * capacity,), jnp.float32).at[slot_index].set(dose_now)]
    pallas_call x0 -> x5, Pallas kernels: none -> 18 us  [the longest x1 7.2 us: per_device(): call(first_kernel, [(3 * CY, CX), (3 * CY, CX), edge, edge], 2, (a_scratc...]
    sub x2 -> x0, other arithmetic: 15.8 us -> none  [the longest x1 15.7 us: per_device(): jnp.arange(shot_count, dtype=jnp.int32) - owner_start[sorted_owner]]
    all_to_all x2 -> x1, starting transfers between devices: 20.4 us -> 11.3 us  [per_device(): recv = lax.all_to_all(send, 'row', split_axis=0, concat_axis=0, tiled=True)]
  transfers between devices with their start and end apart: 10 -> 5, of which waited for: 5 -> 5; matrix products, arithmetic and copies ran while one was open for 2% -> 0% of each run, Pallas kernels for 0% -> 0%
where the time goes in v1:
time: 65.7 us; the launch traced here: 65.3 us
  Pallas kernels  18 us (27%)
  waiting for transfers between devices  17.6 us (27%)
  starting transfers between devices  14.4 us (22%)
  blocking collectives  11.7 us (18%)
  local copies, waits for them, and re-layouts  2.8 us (4%)
  between operations  0.7 us (1%)
    all_to_all x1, blocking collectives, per_device(): back = lax.all_to_all(final, 'row', split_axis=0, concat_axis=0, tiled=True)  11.7 us
    all_to_all x1, starting transfers between devices, per_device(): recv = lax.all_to_all(send, 'row', split_axis=0, concat_axis=0, tiled=True)  11.3 us
    all_to_all x1, waiting for transfers between devices, per_device(): recv = lax.all_to_all(send, 'row', split_axis=0, concat_axis=0, tiled=True)  9.59 us
    pallas_call x1, Pallas kernels, per_device(): call(first_kernel, [(3 * CY, CX), (3 * CY, CX), edge, edge], 2, (a_scratc...  7.2 us
    pallas_call x1, Pallas kernels, per_device(): call(second_kernel, [(N_ROW, CAP), (CY, CX), (CY, CX), edge, edge], 8, (a...  6.69 us
    ppermute x2, waiting for transfers between devices, exchanged(): lax.ppermute(to_left, 'col', [((i + 1) % n, i) for i in range(n)])  6.6 us
    unnamed x16, local copies, waits for them, and re-layouts  2.8 us
    ppermute x2, starting transfers between devices, exchanged(): lax.ppermute(to_right, 'col', [(i, (i + 1) % n) for i in range(n)])  2.59 us
  transfers between devices with their start and end apart: 5, of which 5 were waited for; matrix products, arithmetic and copies ran while one was open for 0% of the time, Pallas kernels for 0%

profile of v1, /device:TPU:7, one launch (start us, length us, event | category | flops | bytes accessed | tf_op | source)
XLA Modules:
  0.0 65.3 jit_solution(6567608499508796310)
XLA Ops:
  0.6 0.0 copy-start.3
  0.6 0.7 %copy-done.3 = s32[2048,1]{0,1:T(1,128)S(1)} copy-done((s32[2048,1]{0,1:T(1,128)S(1)}, s32[2048,1]{0,1:T(1,128)}, u32[]{:S(2)}) %copy-start.3) | copy-done | bytes 8216
  1.3 0.0 copy-start.5
  1.3 0.7 %copy-done.5 = f32[2048]{0:T(1024)S(1)} copy-done((f32[2048]{0:T(1024)S(1)}, f32[2048]{0:T(1024)}, u32[]{:S(2)}) %copy-start.5) | copy-done | bytes 8216
  2.0 0.0 copy-start.6
  2.0 0.7 %copy-done.6 = s32[2048]{0:T(1024)S(1)} copy-done((s32[2048]{0:T(1024)S(1)}, s32[2048]{0:T(1024)}, u32[]{:S(2)}) %copy-start.6) | copy-done | bytes 8216
  2.7 0.0 copy-start.7
  2.7 0.7 %copy-done.7 = s32[2048]{0:T(1024)S(1)} copy-done((s32[2048]{0:T(1024)S(1)}, s32[2048]{0:T(1024)}, u32[]{:S(2)}) %copy-start.7) | copy-done | bytes 8216
  3.4 1.4 %shard_map.86 = (f32[32,1,1280]{2,1,0:T(1,128)}, f32[1,2048]{1,0:T(1,128)S(1)}) custom-call(f32[1,2048]{1,0:T(1,128)S(1)} %bitcast.9, s32[1,2048]{1,0:T(1,128)S(1)} %bitcast.7, s32[1,2048]{1,0:T(1,128)S(1)} %bitcast.10, s32[1,2048]{1,0:T(1,128)S(1)} %bitcast.11), custom_call_target="tpu_custom_call" | custom-call | tf_op jit(solution)/shard_map/pallas_call | solution.py:332
  4.8 0.0 copy-start.1
  4.8 11.3 %all-to-all-start = ((f32[32,1,1280]{2,1,0:T(1,128)}), f32[32,1,1280]{2,1,0:T(1,128)S(1)}, u32[]{:S(2)}, u32[]{:S(2)}) async-start(f32[32,1,1280]{2,1,0:T(1,128)} %get-tuple-element.15), calls=%async_computation | async-start | bytes 327680 | tf_op jit(solution)/shard_map/all_to_all | solution.py:335
  16.2 0.0 copy-start
  16.2 9.6 %all-to-all-done.recv_ref = f32[32,1,1280]{2,1,0:T(1,128)S(1)} async-done(((f32[32,1,1280]{2,1,0:T(1,128)}), f32[32,1,1280]{2,1,0:T(1,128)S(1)}, u32[]{:S(2)}, u32[]{:S(2)}) %all-to-all-start) | async-done | bytes 163872 | tf_op jit(solution)/shard_map/all_to_all | solution.py:335
  25.8 0.0 copy-done.1
  25.8 0.0 copy-start.2
  25.8 7.2 %shard_map.87 = (f32[96,512]{1,0:T(8,128)S(1)}, f32[96,512]{1,0:T(8,128)S(1)}, f32[24,128]{1,0:T(8,128)S(1)}, f32[24,128]{1,0:T(8,128)S(1)}) custom-call(f32[32,1,1280]{2,1,0:T(1,128)S(1)} %all-to-all-done.recv_ref, bf16[192,320]{1,0:T(8,128)(2,1)S(1)} %copy-done.1), custom_call_target="tpu_custom_call" | custom-call | tf_op jit(solution)/shard_map/pallas_call | solution.py:338
  33.0 2.5 %collective-permute-start = (f32[24,128]{1,0:T(8,128)S(1)}, f32[24,128]{1,0:T(8,128)S(1)}, u32[]{:S(2)}, u32[]{:S(2)}) collective-permute-start(f32[24,128]{1,0:T(8,128)S(1)} %get-tuple-element.18), channel_id=1, source_target_pairs={{0,1},{1,2},{2,3},{3,4},{4,5},{5,6},{6,7},{7,0},{8,9},{9,10},{10,1... | collective-permute-start | bytes 36872 | tf_op jit(solution)/shard_map/ppermute | solution.py:320
  35.6 0.0 collective-permute-start.1
  35.6 0.1 add_convert_fusion.sides_ref
  35.6 0.8 %collective-permute-done.from_left_ref = f32[24,128]{1,0:T(8,128)S(1)} collective-permute-done((f32[24,128]{1,0:T(8,128)S(1)}, f32[24,128]{1,0:T(8,128)S(1)}, u32[]{:S(2)}, u32[]{:S(2)}) %collective-permute-start) | collective-permute-done | bytes 12320 | tf_op jit(solution)/shard_map/ppermute | solution.py:320
  36.4 3.5 %collective-permute-done.1.from_right_ref = f32[24,128]{1,0:T(8,128)S(1)} collective-permute-done((f32[24,128]{1,0:T(8,128)S(1)}, f32[24,128]{1,0:T(8,128)S(1)}, u32[]{:S(2)}, u32[]{:S(2)}) %collective-permute-start.1) | collective-permute-done | bytes 12320 | tf_op jit(solution)/shard_map/ppermute | solution.py:321
  39.9 0.0 copy-done
  39.9 0.0 copy-done.2
  39.9 6.7 %shard_map.88 = (f32[32,128]{1,0:T(8,128)S(1)}, f32[32,512]{1,0:T(8,128)S(1)}, f32[32,512]{1,0:T(8,128)S(1)}, f32[8,128]{1,0:T(8,128)S(1)}, f32[8,128]{1,0:T(8,128)S(1)}) custom-call(f32[2]{0:T(128)S(1)} %add_convert_fusion.sides_ref, f32[32,1,1280]{2,1,0:T(1,128)S(1)} %all-to-all-done.recv_ref, f32[96,512]{1,0:T(8,128)S(1)} %get-tuple-element.16.along_ref, ...), custom_call_target="tpu_custom_call" | custom-call | tf_op jit(solution)/shard_map/pallas_call | solution.py:343
  46.6 0.1 collective-permute-start.2
  46.6 0.5 collective-permute-start.3
  47.1 0.7 %collective-permute-done.2.from_left_ref = f32[8,128]{1,0:T(8,128)S(1)} collective-permute-done((f32[8,128]{1,0:T(8,128)S(1)}, f32[8,128]{1,0:T(8,128)S(1)}, u32[]{:S(2)}, u32[]{:S(2)}) %collective-permute-start.2) | collective-permute-done | bytes 4128 | tf_op jit(solution)/shard_map/ppermute | solution.py:320
  47.8 3.1 %collective-permute-done.3.from_right_ref = f32[8,128]{1,0:T(8,128)S(1)} collective-permute-done((f32[8,128]{1,0:T(8,128)S(1)}, f32[8,128]{1,0:T(8,128)S(1)}, u32[]{:S(2)}, u32[]{:S(2)}) %collective-permute-start.3) | collective-permute-done | bytes 4128 | tf_op jit(solution)/shard_map/ppermute | solution.py:321
  50.9 1.8 %shard_map.89 = (f32[32,512]{1,0:T(8,128)}, f32[32,1,128]{2,1,0:T(1,128)S(1)}) custom-call(f32[2]{0:T(128)S(1)} %add_convert_fusion.sides_ref, f32[32,1,1280]{2,1,0:T(1,128)S(1)} %all-to-all-done.recv_ref, f32[32,128]{1,0:T(8,128)S(1)} %get-tuple-element.20.dose_ref, f32[32,512]{1,0:T(8,128)S(1)} %get-tuple-element.21.along_ref, ...), custom_call_target="tpu_custom_call" | custom-call | tf_op jit(solution)/shard_map/pallas_call | solution.py:347
  52.7 0.0 copy-start.4
  52.7 11.7 %all_to_all.10.ret_ref = f32[32,1,128]{2,1,0:T(1,128)S(1)} all-to-all(f32[32,1,128]{2,1,0:T(1,128)S(1)} %get-tuple-element.25), channel_id=1, replica_groups=mesh['row'=32,'col'=8] {'row'}, dimensions={0} | all-to-all | bytes 32768 | tf_op jit(solution)/shard_map/all_to_all | solution.py:350
  64.4 0.0 copy-done.4
  64.4 0.9 %shard_map.90 = f32[1,2048]{1,0:T(1,128)} custom-call(f32[32,1,128]{2,1,0:T(1,128)S(1)} %all_to_all.10.ret_ref, s32[1,2048]{1,0:T(1,128)S(1)} %bitcast.8, f32[1,2048]{1,0:T(1,128)S(1)} %get-tuple-element.26.rank_ref), custom_call_target="tpu_custom_call" | custom-call | tf_op jit(solution)/shard_map/pallas_call | solution.py:351
Async XLA Ops:
  0.6 0.7 %copy-start.3 = (s32[2048,1]{0,1:T(1,128)S(1)}, s32[2048,1]{0,1:T(1,128)}, u32[]{:S(2)}) copy-start(s32[2048,1]{0,1:T(1,128)} %param.8) | copy-start | bytes 24580
  1.3 0.7 %copy-start.5 = (f32[2048]{0:T(1024)S(1)}, f32[2048]{0:T(1024)}, u32[]{:S(2)}) copy-start(f32[2048]{0:T(1024)} %param.7) | copy-start | bytes 24580
  2.0 0.7 %copy-start.6 = (s32[2048]{0:T(1024)S(1)}, s32[2048]{0:T(1024)}, u32[]{:S(2)}) copy-start(s32[2048]{0:T(1024)} %param.9) | copy-start | bytes 24580
  2.7 0.7 %copy-start.7 = (s32[2048]{0:T(1024)S(1)}, s32[2048]{0:T(1024)}, u32[]{:S(2)}) copy-start(s32[2048]{0:T(1024)} %param.10) | copy-start | bytes 24580
  4.8 21.0 %copy-start.1 = (bf16[192,320]{1,0:T(8,128)(2,1)S(1)}, bf16[192,320]{1,0:T(8,128)(2,1)}, u32[]{:S(2)}) copy-start(bf16[192,320]{1,0:T(8,128)(2,1)} %constant.14.clone.ltaps_ref) | copy-start | bytes 368644
  4.8 21.0 %all-to-all-start = ((f32[32,1,1280]{2,1,0:T(1,128)}), f32[32,1,1280]{2,1,0:T(1,128)S(1)}, u32[]{:S(2)}, u32[]{:S(2)}) async-start(f32[32,1,1280]{2,1,0:T(1,128)} %get-tuple-element.15), calls=%async_computation | async-start | bytes 327680 | tf_op jit(solution)/shard_map/all_to_all | solution.py:335
  16.2 23.7 %copy-start = (bf16[384,256]{1,0:T(8,128)(2,1)S(1)}, bf16[384,256]{1,0:T(8,128)(2,1)}, u32[]{:S(2)}) copy-start(bf16[384,256]{1,0:T(8,128)(2,1)} %constant.16.clone.rtaps_ref) | copy-start | bytes 589828
  25.8 14.1 %copy-start.2 = (bf16[64,192]{1,0:T(8,128)(2,1)S(1)}, bf16[64,192]{1,0:T(8,128)(2,1)}, u32[]{:S(2)}) copy-start(bf16[64,192]{1,0:T(8,128)(2,1)} %constant.15.clone.ltaps_ref) | copy-start | bytes 73732
  33.0 3.4 %collective-permute-start = (f32[24,128]{1,0:T(8,128)S(1)}, f32[24,128]{1,0:T(8,128)S(1)}, u32[]{:S(2)}, u32[]{:S(2)}) collective-permute-start(f32[24,128]{1,0:T(8,128)S(1)} %get-tuple-element.18), channel_id=1, source_target_pairs={{0,1},{1,2},{2,3},{3,4},{4,5},{5,6},{6,7},{7,0},{8,9},{9,10},{10,1... | collective-permute-start | bytes 36872 | tf_op jit(solution)/shard_map/ppermute | solution.py:320
  35.6 4.3 %collective-permute-start.1 = (f32[24,128]{1,0:T(8,128)S(1)}, f32[24,128]{1,0:T(8,128)S(1)}, u32[]{:S(2)}, u32[]{:S(2)}) collective-permute-start(f32[24,128]{1,0:T(8,128)S(1)} %get-tuple-element.19), channel_id=1, source_target_pairs={{1,0},{2,1},{3,2},{4,3},{5,4},{6,5},{7,6},{0,7},{9,8},{10,9},{11,1... | collective-permute-start | bytes 36872 | tf_op jit(solution)/shard_map/ppermute | solution.py:321
  46.6 1.2 %collective-permute-start.2 = (f32[8,128]{1,0:T(8,128)S(1)}, f32[8,128]{1,0:T(8,128)S(1)}, u32[]{:S(2)}, u32[]{:S(2)}) collective-permute-start(f32[8,128]{1,0:T(8,128)S(1)} %get-tuple-element.23), channel_id=1, source_target_pairs={{0,1},{1,2},{2,3},{3,4},{4,5},{5,6},{6,7},{7,0},{8,9},{9,10},{10,1... | collective-permute-start | bytes 12296 | tf_op jit(solution)/shard_map/ppermute | solution.py:320
  46.6 4.2 %collective-permute-start.3 = (f32[8,128]{1,0:T(8,128)S(1)}, f32[8,128]{1,0:T(8,128)S(1)}, u32[]{:S(2)}, u32[]{:S(2)}) collective-permute-start(f32[8,128]{1,0:T(8,128)S(1)} %get-tuple-element.24), channel_id=1, source_target_pairs={{1,0},{2,1},{3,2},{4,3},{5,4},{6,5},{7,6},{0,7},{9,8},{10,9},{11,1... | collective-permute-start | bytes 12296 | tf_op jit(solution)/shard_map/ppermute | solution.py:321
  52.7 11.7 %copy-start.4 = (s32[2048,1]{0,1:T(1,128)S(1)}, s32[2048,1]{0,1:T(1,128)}, u32[]{:S(2)}) copy-start(s32[2048,1]{0,1:T(1,128)} %param.8) | copy-start | bytes 24580

commit v2 on v1

--- a/solution.py
+++ b/solution.py
@@ -19,6 +19,7 @@
 NB = CX // BLK
 XR = BLK + 16
 SLOTS = N_ROW * CAP
+SUB16 = 16
 BF = jnp.bfloat16
 F32 = jnp.float32
 
@@ -124,40 +125,64 @@
     off_y = jnp.floor(fine * (1.0 / 16.0))
     off_x = fine - 16.0 * off_y
     block = jnp.floor(cell_x * (1.0 / BLK))
-    return block, cell_y, cell_x - BLK * block, off_y * (1.0 / 16.0), off_x * (1.0 / 16.0)
-
-
-def over_rows(v, rows):
-    return jnp.broadcast_to(v, (rows, v.shape[1])).astype(BF)
-
-
-def build_columns(column, off_x, b_ref, rows0):
-    for i in range(N_ROW):
-        here = slice(i * CAP, (i + 1) * CAP)
-        at = lax.broadcasted_iota(jnp.int32, (XR, CAP), 0).astype(F32).astype(BF)
-        first = over_rows(column[i:i + 1], XR)
-        second = over_rows(column[i:i + 1] + 1.0, XR)
-        w0 = over_rows(1.0 - off_x[i:i + 1], XR)
-        w1 = over_rows(off_x[i:i + 1], XR)
-        b_ref[rows0:rows0 + XR, here] = jnp.where(at == first, w0, jnp.where(at == second, w1, jnp.zeros_like(w0)))
-
-
-def build_rows(key, off_y, dose, a_ref):
-    hi0, lo0 = split2((1.0 - off_y) * dose)
-    hi1, lo1 = split2(off_y * dose)
-    hi0, lo0, hi1, lo1 = (v.astype(F32) for v in (hi0, lo0, hi1, lo1))
-    for i in range(N_ROW):
-        here = slice(i * CAP, (i + 1) * CAP)
-        at = lax.broadcasted_iota(jnp.int32, (BLK, CAP), 0).astype(F32).astype(BF)
-        first = at == over_rows(key[i:i + 1], BLK)
-        second = at == over_rows(key[i:i + 1] + 1.0, BLK)
-        for part, (p0, p1) in enumerate(((hi0, hi1), (lo0, lo1))):
-            q0, q1 = over_rows(p0[i:i + 1], BLK), over_rows(p1[i:i + 1], BLK)
-            a_ref[part * BLK:(part + 1) * BLK, here] = jnp.where(first, q0, jnp.where(second, q1, jnp.zeros_like(q0)))
-
-
-def tile_density(a, b):
-    both = nt_dot(a, b)
+    column = cell_x - BLK * block
+    off_y, off_x = off_y * (1.0 / 16.0), off_x * (1.0 / 16.0)
+    return dict(block=block, y=cell_y, y1=cell_y + 1.0, column=column, column1=column + 1.0,
+                y0w=1.0 - off_y, y1w=off_y, x0=1.0 - off_x, x1=off_x)
+
+
+def pair_columns(shot):
+    return lambda i: jnp.concatenate([column_chunk(shot, i), column_chunk(shot, i + 1)], 1)
+
+
+def over_rows(v, i):
+    return jnp.broadcast_to(v[i:i + 1], (SUB16, CAP)).astype(BF)
+
+
+def row_numbers(first):
+    return (lax.broadcasted_iota(jnp.int32, (SUB16, CAP), 0) + first).astype(F32).astype(BF)
+
+
+def column_chunk(shot, i):
+    first, second = over_rows(shot["column"], i), over_rows(shot["column1"], i)
+    w0, w1 = over_rows(shot["x0"], i), over_rows(shot["x1"], i)
+    none = jnp.zeros_like(w0)
+    out = []
+    for k in range(XR // SUB16):
+        at = row_numbers(SUB16 * k)
+        out.append(jnp.where(at == first, w0, jnp.where(at == second, w1, none)))
+    return jnp.concatenate(out, 0)
+
+
+def row_chunk(shot, dosed, i):
+    first, second = over_rows(shot["y"], i), over_rows(shot["y1"], i)
+    block = over_rows(shot["block"], i)
+    values = [over_rows(v, i) for v in dosed]
+    none = jnp.zeros_like(first)
+    parts = [[], []]
+    for k in range(CY // SUB16):
+        at = row_numbers(SUB16 * k)
+        on_first, on_second = at == first, at == second
+        for part in range(2):
+            q0, q1 = values[2 * part:2 * part + 2]
+            parts[part].append(jnp.where(on_first, q0, jnp.where(on_second, q1, none)))
+    inside = [block == jnp.full((SUB16, CAP), h, F32).astype(BF) for h in range(NB)]
+    return jnp.concatenate([jnp.where(inside[h], v, none) for part in parts for h in range(NB) for v in part], 0)
+
+
+def dosed_weights(shot, dose):
+    hi0, lo0 = split2(shot["y0w"] * dose)
+    hi1, lo1 = split2(shot["y1w"] * dose)
+    return [v.astype(F32) for v in (hi0, hi1, lo0, lo1)]
+
+
+def tile_density(shot, dose, columns):
+    dosed = dosed_weights(shot, dose)
+    both = None
+    for i in range(0, N_ROW, 2):
+        a = jnp.concatenate([row_chunk(shot, dosed, i), row_chunk(shot, dosed, i + 1)], 1)
+        one = nt_dot(a, columns(i))
+        both = one if both is None else both + one
     d = both[:BLK] + both[BLK:]
     blocks = [d[:CY, :BLK]]
     for h in range(1, NB):
@@ -205,7 +230,7 @@
     return jnp.concatenate([out[h * rows:(h + 1) * rows] for h in range(NB)], 1)
 
 
-def gathered(total, key_block, cell_y, off_y, b):
+def gathered(total, shot, b_ref):
     pieces = []
     for h in range(NB):
         inside = total[:, h * BLK:(h + 1) * BLK]
@@ -215,19 +240,24 @@
             after = jnp.zeros((CY, XR - BLK), F32)
         pieces.append(jnp.concatenate([inside, after], 1))
     hi, lo = split2(jnp.concatenate(pieces, 0))
-    both = nn_dot(jnp.concatenate([hi, lo], 0), b)
+    table = jnp.concatenate([hi, lo], 0)
     at = lax.broadcasted_iota(jnp.int32, (CY, CAP), 0).astype(F32)
     rows = []
-    for i in range(N_ROW):
-        here = slice(i * CAP, (i + 1) * CAP)
-        g = both[:BLK, here] + both[BLK:, here]
-        block = key_block[i:i + 1]
-        mine = g[:CY]
-        for h in range(1, NB):
-            mine = jnp.where(block == float(h), g[h * CY:(h + 1) * CY], mine)
-        y, o = cell_y[i:i + 1], off_y[i:i + 1]
-        w = jnp.where(at == y, 1.0 - o, jnp.where(at == y + 1.0, o, 0.0))
-        rows.append(jnp.sum(w * mine, axis=0, keepdims=True))
+    for i in range(0, N_ROW, 2):
+        columns = pair_columns(shot)(i)
+        if b_ref is not None:
+            b_ref[:, i * CAP:(i + 2) * CAP] = columns
+        both = nn_dot(table, columns)
+        for j in range(2):
+            here = slice(j * CAP, (j + 1) * CAP)
+            g = both[:BLK, here] + both[BLK:, here]
+            block = shot["block"][i + j:i + j + 1]
+            mine = g[:CY]
+            for h in range(1, NB):
+                mine = jnp.where(block == float(h), g[h * CY:(h + 1) * CY], mine)
+            y, y1 = shot["y"][i + j:i + j + 1], shot["y1"][i + j:i + j + 1]
+            w = jnp.where(at == y, shot["y0w"][i + j:i + j + 1], jnp.where(at == y1, shot["y1w"][i + j:i + j + 1], 0.0))
+            rows.append(jnp.sum(w * mine, axis=0, keepdims=True))
     return jnp.concatenate(rows, 0)
 
 
@@ -235,15 +265,17 @@
     return jnp.where(dose > 0.0, dose * (1.0 + BACKSCATTER) / exposure, 0.0)
 
 
-def first_kernel(recv_ref, ltaps_ref, along_ref, density_ref, to_left_ref, to_right_ref, a_ref, b_ref):
+def slots(recv_ref, t):
+    start = 2 * t * CAP
+    return recv_ref[:, 0, start:start + CAP], recv_ref[:, 0, start + CAP:start + 2 * CAP]
+
+
+def first_kernel(recv_ref, ltaps_ref, along_ref, density_ref, to_left_ref, to_right_ref):
     tiles = []
     for t in range(NT):
-        place = recv_ref[:, 0, 2 * t * CAP:(2 * t + 1) * CAP]
-        dose = recv_ref[:, 0, (2 * t + 1) * CAP:(2 * t + 2) * CAP]
-        block, cell_y, column, off_y, off_x = decoded(place)
-        build_columns(column, off_x, b_ref, 0)
-        build_rows(block * CY + cell_y, off_y, dose, a_ref)
-        tiles.append(tile_density(a_ref[...], b_ref[...]))
+        place, dose = slots(recv_ref, t)
+        shot = decoded(place)
+        tiles.append(tile_density(shot, dose, pair_columns(shot)))
     density_ref[...] = jnp.concatenate(tiles[1:NT - 1], 0)
     along = blurred_y(jnp.concatenate(tiles, 0), ltaps_ref)
     along_ref[...] = along
@@ -251,25 +283,25 @@
     to_right_ref[...] = packed_edge(along[:, CX - BLK:], BLK - 32)
 
 
-def second_kernel(sides_ref, recv_ref, along_ref, density_ref, from_left_ref, from_right_ref, rtaps_ref, ltaps_ref,
-                  dose_ref, along2_ref, density2_ref, to_left_ref, to_right_ref, a_ref, b_ref):
-    left = unpacked_edge(from_left_ref[...] * sides_ref[0], BLK - 32)
-    right = unpacked_edge(from_right_ref[...] * sides_ref[1], 0)
-    field = blurred_x(along_ref[...], left, right, rtaps_ref)
-    total = density_ref[...] + BACKSCATTER * field
+def field_of(along_ref, from_left_ref, from_right_ref, rtaps_ref):
+    col = lax.axis_index("col")
+    left = unpacked_edge(jnp.where(col > 0, from_left_ref[...], 0.0), BLK - 32)
+    right = unpacked_edge(jnp.where(col < N_COL - 1, from_right_ref[...], 0.0), 0)
+    return blurred_x(along_ref[...], left, right, rtaps_ref)
+
+
+def second_kernel(recv_ref, along_ref, density_ref, from_left_ref, from_right_ref, rtaps_ref, ltaps_ref,
+                  dose_ref, along2_ref, density2_ref, to_left_ref, to_right_ref, b_ref):
+    total = density_ref[...] + BACKSCATTER * field_of(along_ref, from_left_ref, from_right_ref, rtaps_ref)
     tiles = []
     for n in range(NT - 2):
-        t = n + 1
-        place = recv_ref[:, 0, 2 * t * CAP:(2 * t + 1) * CAP]
-        dose = recv_ref[:, 0, (2 * t + 1) * CAP:(2 * t + 2) * CAP]
-        block, cell_y, column, off_y, off_x = decoded(place)
-        build_columns(column, off_x, b_ref, 0)
-        exposure = gathered(total[n * CY:(n + 1) * CY], block, cell_y, off_y, b_ref[...])
+        place, dose = slots(recv_ref, n + 1)
+        shot = decoded(place)
+        exposure = gathered(total[n * CY:(n + 1) * CY], shot, b_ref)
         dose = corrected(dose, exposure)
-        if t == REACH:
+        if n + 1 == REACH:
             dose_ref[...] = dose
-        build_rows(block * CY + cell_y, off_y, dose, a_ref)
-        tiles.append(tile_density(a_ref[...], b_ref[...]))
+        tiles.append(tile_density(shot, dose, lambda i: b_ref[:, i * CAP:(i + 2) * CAP]))
     density2_ref[...] = tiles[1]
     along = blurred_y(jnp.concatenate(tiles, 0), ltaps_ref)
     along2_ref[...] = along
@@ -277,17 +309,11 @@
     to_right_ref[...] = packed_edge(along[:, CX - BLK:], BLK - 32)
 
 
-def third_kernel(sides_ref, recv_ref, dose_ref, along_ref, density_ref, from_left_ref, from_right_ref, rtaps_ref,
-                 field_ref, final_ref, b_ref):
-    left = unpacked_edge(from_left_ref[...] * sides_ref[0], BLK - 32)
-    right = unpacked_edge(from_right_ref[...] * sides_ref[1], 0)
-    field = blurred_x(along_ref[...], left, right, rtaps_ref)
+def third_kernel(recv_ref, dose_ref, along_ref, density_ref, from_left_ref, from_right_ref, rtaps_ref, field_ref, final_ref):
+    field = field_of(along_ref, from_left_ref, from_right_ref, rtaps_ref)
     field_ref[...] = field
-    total = density_ref[...] + BACKSCATTER * field
-    place = recv_ref[:, 0, 2 * REACH * CAP:(2 * REACH + 1) * CAP]
-    block, cell_y, column, off_y, off_x = decoded(place)
-    build_columns(column, off_x, b_ref, 0)
-    exposure = gathered(total, block, cell_y, off_y, b_ref[...])
+    place, _ = slots(recv_ref, REACH)
+    exposure = gathered(density_ref[...] + BACKSCATTER * field, decoded(place), None)
     final_ref[:, 0, :] = corrected(dose_ref[...], exposure)
 
 
@@ -304,11 +330,11 @@
     return pl.BlockSpec(memory_space=pltpu.VMEM)
 
 
-def call(kernel, outs, n_in, scratch=(), scalars=0):
+def call(kernel, outs, n_in, scratch=()):
     return pl.pallas_call(
         kernel,
         out_shape=[jax.ShapeDtypeStruct(s, F32) for s in outs],
-        in_specs=[pl.BlockSpec(memory_space=pltpu.SMEM)] * scalars + [vmem()] * (n_in - scalars),
+        in_specs=[vmem()] * n_in,
         out_specs=[vmem() for _ in outs],
         scratch_shapes=list(scratch),
         compiler_params=pltpu.CompilerParams(vmem_limit_bytes=48 << 20),
@@ -323,8 +349,6 @@
 
 
 def per_device(shot_dose, shot_owner, shot_cell, shot_offset):
-    col = lax.axis_index("col")
-    sides = jnp.stack([col > 0, col < N_COL - 1]).astype(F32)
     owner = shot_owner.reshape(1, S_DEV)
     ltaps = jnp.asarray(left_constant(3 * CY, NT * CY, CY))
     ltaps2 = jnp.asarray(left_constant(CY, 3 * CY, CY))
@@ -333,19 +357,16 @@
         shot_dose.reshape(1, S_DEV), owner, shot_cell.reshape(1, S_DEV), shot_offset.reshape(1, S_DEV)
     )
     recv = lax.all_to_all(send, "row", split_axis=0, concat_axis=0, tiled=True)
-    a_scratch, b_scratch = pltpu.VMEM((2 * BLK, SLOTS), BF), pltpu.VMEM((XR, SLOTS), BF)
     edge = (3 * CY // 4, BLK)
-    along, density, to_left, to_right = call(
-        first_kernel, [(3 * CY, CX), (3 * CY, CX), edge, edge], 2, (a_scratch, b_scratch)
-    )(recv, ltaps)
+    along, density, to_left, to_right = call(first_kernel, [(3 * CY, CX), (3 * CY, CX), edge, edge], 2)(recv, ltaps)
     from_left, from_right = exchanged(to_left, to_right)
     edge = (CY // 4, BLK)
     dose, along, density, to_left, to_right = call(
-        second_kernel, [(N_ROW, CAP), (CY, CX), (CY, CX), edge, edge], 8, (a_scratch, b_scratch), 1
-    )(sides, recv, along, density, from_left, from_right, rtaps, ltaps2)
+        second_kernel, [(N_ROW, CAP), (CY, CX), (CY, CX), edge, edge], 7, (pltpu.VMEM((XR, SLOTS), BF),)
+    )(recv, along, density, from_left, from_right, rtaps, ltaps2)
     from_left, from_right = exchanged(to_left, to_right)
-    field, final = call(third_kernel, [(CY, CX), (N_ROW, 1, CAP)], 8, (b_scratch,), 1)(
-        sides, recv, dose, along, density, from_left, from_right, rtaps
+    field, final = call(third_kernel, [(CY, CX), (N_ROW, 1, CAP)], 7)(
+        recv, dose, along, density, from_left, from_right, rtaps
     )
     back = lax.all_to_all(final, "row", split_axis=0, concat_axis=0, tiled=True)
     (out,) = call(unpack_kernel, [(1, S_DEV)], 3)(back, owner, rank)

time: 65.7 us -> 58.7 us (0.89)
  blocking collectives: 11.7 us -> 32.4 us
  starting transfers between devices: 14.4 us -> 3.07 us
  waiting for transfers between devices: 17.6 us -> 8.09 us
  Pallas kernels: 18 us -> 11.2 us
    all_to_all x0 -> x1, blocking collectives: none -> 20.8 us  [per_device(): recv = lax.all_to_all(send, 'row', split_axis=0, concat_axis=0, tiled=True)]
    all_to_all x1 -> x0, starting transfers between devices: 11.3 us -> none  [per_device(): recv = lax.all_to_all(send, 'row', split_axis=0, concat_axis=0, tiled=True)]
    all_to_all x1 -> x0, waiting for transfers between devices: 9.59 us -> none  [per_device(): recv = lax.all_to_all(send, 'row', split_axis=0, concat_axis=0, tiled=True)]
    pallas_call x3, Pallas kernels: 15.7 us -> 9.55 us  [the longest x1 4.89 us: per_device(): call(second_kernel, [(N_ROW, CAP), (CY, CX), (CY, CX), edge, edge], 7, (p...]
    pallas_call x1, Pallas kernels: 1.42 us -> 0.75 us  [per_device(): call(pack_kernel, [(N_ROW, 1, 2 * NT * CAP), (1, S_DEV)], 4)]
  transfers between devices with their start and end apart: 5 -> 4, of which waited for: 5 -> 4; matrix products, arithmetic and copies ran while one was open for 0% -> 0% of each run, Pallas kernels for 0% -> 0%
where the time goes in v2:
time: 58.7 us; the launch traced here: 58.3 us
  blocking collectives  32.4 us (55%)
  Pallas kernels  11.2 us (19%)
  waiting for transfers between devices  8.09 us (14%)
  starting transfers between devices  3.07 us (5%)
  local copies, waits for them, and re-layouts  2.8 us (5%)
  between operations  0.69 us (1%)
    all_to_all x1, blocking collectives, per_device(): recv = lax.all_to_all(send, 'row', split_axis=0, concat_axis=0, tiled=True)  20.8 us
    all_to_all x1, blocking collectives, per_device(): back = lax.all_to_all(final, 'row', split_axis=0, concat_axis=0, tiled=True)  11.7 us
    ppermute x2, waiting for transfers between devices, exchanged(): lax.ppermute(to_left, 'col', [((i + 1) % n, i) for i in range(n)])  6.61 us
    pallas_call x1, Pallas kernels, per_device(): call(second_kernel, [(N_ROW, CAP), (CY, CX), (CY, CX), edge, edge], 7, (p...  4.89 us
    pallas_call x1, Pallas kernels, per_device(): call(first_kernel, [(3 * CY, CX), (3 * CY, CX), edge, edge], 2)(recv, ltaps)  3.56 us
    unnamed x16, local copies, waits for them, and re-layouts  2.8 us
    ppermute x2, starting transfers between devices, exchanged(): lax.ppermute(to_right, 'col', [(i, (i + 1) % n) for i in range(n)])  2.59 us
    ppermute x2, waiting for transfers between devices, exchanged(): lax.ppermute(to_right, 'col', [(i, (i + 1) % n) for i in range(n)])  1.48 us
  transfers between devices with their start and end apart: 4, of which 4 were waited for; matrix products, arithmetic and copies ran while one was open for 0% of the time, Pallas kernels for 0%

profile of v2, /device:TPU:7, one launch (start us, length us, event | category | flops | bytes accessed | tf_op | source)
XLA Modules:
  0.0 58.3 jit_solution(13318432802062486658)
XLA Ops:
  0.6 0.0 copy-start.3
  0.6 0.7 %copy-done.3 = s32[2048,1]{0,1:T(1,128)S(1)} copy-done((s32[2048,1]{0,1:T(1,128)S(1)}, s32[2048,1]{0,1:T(1,128)}, u32[]{:S(2)}) %copy-start.3) | copy-done | bytes 8216
  1.3 0.0 copy-start.5
  1.3 0.7 %copy-done.5 = f32[2048]{0:T(1024)S(1)} copy-done((f32[2048]{0:T(1024)S(1)}, f32[2048]{0:T(1024)}, u32[]{:S(2)}) %copy-start.5) | copy-done | bytes 8216
  2.0 0.0 copy-start.6
  2.0 0.7 %copy-done.6 = s32[2048]{0:T(1024)S(1)} copy-done((s32[2048]{0:T(1024)S(1)}, s32[2048]{0:T(1024)}, u32[]{:S(2)}) %copy-start.6) | copy-done | bytes 8216
  2.7 0.0 copy-start.7
  2.7 0.7 %copy-done.7 = s32[2048]{0:T(1024)S(1)} copy-done((s32[2048]{0:T(1024)S(1)}, s32[2048]{0:T(1024)}, u32[]{:S(2)}) %copy-start.7) | copy-done | bytes 8216
  3.4 0.7 %shard_map.86 = (f32[32,1,1280]{2,1,0:T(1,128)S(1)}, f32[1,2048]{1,0:T(1,128)S(1)}) custom-call(f32[1,2048]{1,0:T(1,128)S(1)} %bitcast.7, s32[1,2048]{1,0:T(1,128)S(1)} %bitcast.5, s32[1,2048]{1,0:T(1,128)S(1)} %bitcast.8, s32[1,2048]{1,0:T(1,128)S(1)} %bitcast.9), custom_call_target="tpu_custom_call" | custom-call | tf_op jit(solution)/shard_map/pallas_call | solution.py:356
  4.2 0.0 copy-start.1
  4.2 20.8 %all_to_all.10.recv_ref = f32[32,1,1280]{2,1,0:T(1,128)S(1)} all-to-all(f32[32,1,1280]{2,1,0:T(1,128)S(1)} %get-tuple-element.15), channel_id=1, replica_groups=mesh['row'=32,'col'=8] {'row'}, dimensions={0} | all-to-all | bytes 327680 | tf_op jit(solution)/shard_map/all_to_all | solution.py:359
  24.9 0.0 copy-done.1
  24.9 0.0 copy-start
  24.9 0.0 copy-start.2
  24.9 3.6 %shard_map.87 = (f32[96,512]{1,0:T(8,128)S(1)}, f32[96,512]{1,0:T(8,128)S(1)}, f32[24,128]{1,0:T(8,128)S(1)}, f32[24,128]{1,0:T(8,128)S(1)}) custom-call(f32[32,1,1280]{2,1,0:T(1,128)S(1)} %all_to_all.10.recv_ref, bf16[192,320]{1,0:T(8,128)(2,1)S(1)} %copy-done.1), custom_call_target="tpu_custom_call" | custom-call | tf_op jit(solution)/shard_map/pallas_call | solution.py:361
  28.5 2.5 %collective-permute-start = (f32[24,128]{1,0:T(8,128)S(1)}, f32[24,128]{1,0:T(8,128)S(1)}, u32[]{:S(2)}, u32[]{:S(2)}) collective-permute-start(f32[24,128]{1,0:T(8,128)S(1)} %get-tuple-element.18), channel_id=1, source_target_pairs={{0,1},{1,2},{2,3},{3,4},{4,5},{5,6},{6,7},{7,0},{8,9},{9,10},{10,1... | collective-permute-start | bytes 36872 | tf_op jit(solution)/shard_map/ppermute | solution.py:346
  31.0 0.0 collective-permute-start.1
  31.1 0.8 %collective-permute-done.from_left_ref = f32[24,128]{1,0:T(8,128)S(1)} collective-permute-done((f32[24,128]{1,0:T(8,128)S(1)}, f32[24,128]{1,0:T(8,128)S(1)}, u32[]{:S(2)}, u32[]{:S(2)}) %collective-permute-start) | collective-permute-done | bytes 12320 | tf_op jit(solution)/shard_map/ppermute | solution.py:346
  31.9 3.5 %collective-permute-done.1.from_right_ref = f32[24,128]{1,0:T(8,128)S(1)} collective-permute-done((f32[24,128]{1,0:T(8,128)S(1)}, f32[24,128]{1,0:T(8,128)S(1)}, u32[]{:S(2)}, u32[]{:S(2)}) %collective-permute-start.1) | collective-permute-done | bytes 12320 | tf_op jit(solution)/shard_map/ppermute | solution.py:347
  35.4 0.0 copy-done
  35.4 0.0 copy-done.2
  35.4 4.9 %shard_map.88 = (f32[32,128]{1,0:T(8,128)S(1)}, f32[32,512]{1,0:T(8,128)S(1)}, f32[32,512]{1,0:T(8,128)S(1)}, f32[8,128]{1,0:T(8,128)S(1)}, f32[8,128]{1,0:T(8,128)S(1)}) custom-call(f32[32,1,1280]{2,1,0:T(1,128)S(1)} %all_to_all.10.recv_ref, f32[96,512]{1,0:T(8,128)S(1)} %get-tuple-element.16.along_ref, f32[96,512]{1,0:T(8,128)S(1)} %get-tuple-element.17.density_ref, ...), custom_call_target="tpu_custom_call" | custom-call | tf_op jit(solution)/shard_map/pallas_call | solution.py:364
  40.3 0.1 collective-permute-start.2
  40.3 0.5 collective-permute-start.3
  40.8 0.7 %collective-permute-done.2.from_left_ref = f32[8,128]{1,0:T(8,128)S(1)} collective-permute-done((f32[8,128]{1,0:T(8,128)S(1)}, f32[8,128]{1,0:T(8,128)S(1)}, u32[]{:S(2)}, u32[]{:S(2)}) %collective-permute-start.2) | collective-permute-done | bytes 4128 | tf_op jit(solution)/shard_map/ppermute | solution.py:346
  41.5 3.1 %collective-permute-done.3.from_right_ref = f32[8,128]{1,0:T(8,128)S(1)} collective-permute-done((f32[8,128]{1,0:T(8,128)S(1)}, f32[8,128]{1,0:T(8,128)S(1)}, u32[]{:S(2)}, u32[]{:S(2)}) %collective-permute-start.3) | collective-permute-done | bytes 4128 | tf_op jit(solution)/shard_map/ppermute | solution.py:347
  44.6 1.1 %shard_map.89 = (f32[32,512]{1,0:T(8,128)}, f32[32,1,128]{2,1,0:T(1,128)S(1)}) custom-call(f32[32,1,1280]{2,1,0:T(1,128)S(1)} %all_to_all.10.recv_ref, f32[32,128]{1,0:T(8,128)S(1)} %get-tuple-element.20.dose_ref, f32[32,512]{1,0:T(8,128)S(1)} %get-tuple-element.21.along_ref, f32[32,512]{1,0:T(8,128)S(1)} %get-tuple-element.22.density_ref, ...), custom_call_target="tpu_custom_call" | custom-call | tf_op jit(solution)/shard_map/pallas_call | solution.py:368
  45.7 0.0 copy-start.4
  45.7 11.7 %all_to_all.11.ret_ref = f32[32,1,128]{2,1,0:T(1,128)S(1)} all-to-all(f32[32,1,128]{2,1,0:T(1,128)S(1)} %get-tuple-element.25), channel_id=1, replica_groups=mesh['row'=32,'col'=8] {'row'}, dimensions={0} | all-to-all | bytes 32768 | tf_op jit(solution)/shard_map/all_to_all | solution.py:371
  57.4 0.0 copy-done.4
  57.4 0.9 %shard_map.90 = f32[1,2048]{1,0:T(1,128)} custom-call(f32[32,1,128]{2,1,0:T(1,128)S(1)} %all_to_all.11.ret_ref, s32[1,2048]{1,0:T(1,128)S(1)} %bitcast.6, f32[1,2048]{1,0:T(1,128)S(1)} %get-tuple-element.26.rank_ref), custom_call_target="tpu_custom_call" | custom-call | tf_op jit(solution)/shard_map/pallas_call | solution.py:372
Async XLA Ops:
  0.6 0.7 %copy-start.3 = (s32[2048,1]{0,1:T(1,128)S(1)}, s32[2048,1]{0,1:T(1,128)}, u32[]{:S(2)}) copy-start(s32[2048,1]{0,1:T(1,128)} %param.8) | copy-start | bytes 24580
  1.3 0.7 %copy-start.5 = (f32[2048]{0:T(1024)S(1)}, f32[2048]{0:T(1024)}, u32[]{:S(2)}) copy-start(f32[2048]{0:T(1024)} %param.7) | copy-start | bytes 24580
  2.0 0.7 %copy-start.6 = (s32[2048]{0:T(1024)S(1)}, s32[2048]{0:T(1024)}, u32[]{:S(2)}) copy-start(s32[2048]{0:T(1024)} %param.9) | copy-start | bytes 24580
  2.7 0.7 %copy-start.7 = (s32[2048]{0:T(1024)S(1)}, s32[2048]{0:T(1024)}, u32[]{:S(2)}) copy-start(s32[2048]{0:T(1024)} %param.10) | copy-start | bytes 24580
  4.2 20.8 %copy-start.1 = (bf16[192,320]{1,0:T(8,128)(2,1)S(1)}, bf16[192,320]{1,0:T(8,128)(2,1)}, u32[]{:S(2)}) copy-start(bf16[192,320]{1,0:T(8,128)(2,1)} %constant.6.clone.ltaps_ref) | copy-start | bytes 368644
  24.9 10.4 %copy-start = (bf16[384,256]{1,0:T(8,128)(2,1)S(1)}, bf16[384,256]{1,0:T(8,128)(2,1)}, u32[]{:S(2)}) copy-start(bf16[384,256]{1,0:T(8,128)(2,1)} %constant.8.clone.rtaps_ref) | copy-start | bytes 589828
  24.9 10.4 %copy-start.2 = (bf16[64,192]{1,0:T(8,128)(2,1)S(1)}, bf16[64,192]{1,0:T(8,128)(2,1)}, u32[]{:S(2)}) copy-start(bf16[64,192]{1,0:T(8,128)(2,1)} %constant.7.clone.ltaps_ref) | copy-start | bytes 73732
  28.5 3.4 %collective-permute-start = (f32[24,128]{1,0:T(8,128)S(1)}, f32[24,128]{1,0:T(8,128)S(1)}, u32[]{:S(2)}, u32[]{:S(2)}) collective-permute-start(f32[24,128]{1,0:T(8,128)S(1)} %get-tuple-element.18), channel_id=1, source_target_pairs={{0,1},{1,2},{2,3},{3,4},{4,5},{5,6},{6,7},{7,0},{8,9},{9,10},{10,1... | collective-permute-start | bytes 36872 | tf_op jit(solution)/shard_map/ppermute | solution.py:346
  31.0 4.3 %collective-permute-start.1 = (f32[24,128]{1,0:T(8,128)S(1)}, f32[24,128]{1,0:T(8,128)S(1)}, u32[]{:S(2)}, u32[]{:S(2)}) collective-permute-start(f32[24,128]{1,0:T(8,128)S(1)} %get-tuple-element.19), channel_id=1, source_target_pairs={{1,0},{2,1},{3,2},{4,3},{5,4},{6,5},{7,6},{0,7},{9,8},{10,9},{11,1... | collective-permute-start | bytes 36872 | tf_op jit(solution)/shard_map/ppermute | solution.py:347
  40.3 1.2 %collective-permute-start.2 = (f32[8,128]{1,0:T(8,128)S(1)}, f32[8,128]{1,0:T(8,128)S(1)}, u32[]{:S(2)}, u32[]{:S(2)}) collective-permute-start(f32[8,128]{1,0:T(8,128)S(1)} %get-tuple-element.23), channel_id=1, source_target_pairs={{0,1},{1,2},{2,3},{3,4},{4,5},{5,6},{6,7},{7,0},{8,9},{9,10},{10,1... | collective-permute-start | bytes 12296 | tf_op jit(solution)/shard_map/ppermute | solution.py:346
  40.3 4.2 %collective-permute-start.3 = (f32[8,128]{1,0:T(8,128)S(1)}, f32[8,128]{1,0:T(8,128)S(1)}, u32[]{:S(2)}, u32[]{:S(2)}) collective-permute-start(f32[8,128]{1,0:T(8,128)S(1)} %get-tuple-element.24), channel_id=1, source_target_pairs={{1,0},{2,1},{3,2},{4,3},{5,4},{6,5},{7,6},{0,7},{9,8},{10,9},{11,1... | collective-permute-start | bytes 12296 | tf_op jit(solution)/shard_map/ppermute | solution.py:347
  45.7 11.7 %copy-start.4 = (s32[2048,1]{0,1:T(1,128)S(1)}, s32[2048,1]{0,1:T(1,128)}, u32[]{:S(2)}) copy-start(s32[2048,1]{0,1:T(1,128)} %param.8) | copy-start | bytes 24580

commit v3 on v2

--- a/solution.py
+++ b/solution.py
@@ -83,31 +83,59 @@
     return jnp.concatenate([v[by:], pad], 0) if by > 0 else jnp.concatenate([pad, v[:by]], 0)
 
 
-def pack_kernel(dose_ref, owner_ref, cell_ref, offset_ref, send_ref, rank_ref):
-    owner = owner_ref[...]
-    place = (cell_ref[...] * 256 + offset_ref[...]).astype(F32)
-    dose = dose_ref[...]
+def repeated(row):
+    return jnp.broadcast_to(row, (SUB16, row.shape[1])).astype(BF)
+
+
+def numbers(first, width):
+    return (lax.broadcasted_iota(jnp.int32, (SUB16, width), 0) + first).astype(F32).astype(BF)
+
+
+def equal_rows(row, rows):
+    wide = repeated(row)
+    return [numbers(SUB16 * k, row.shape[1]) == wide for k in range(rows // SUB16)]
+
+
+def chosen(masks, row):
+    wide = repeated(row)
+    none = jnp.zeros_like(wide)
+    return jnp.concatenate([jnp.where(m, wide, none) for m in masks], 0)
+
+
+def pack_kernel(dose_hbm, owner_hbm, cell_hbm, offset_hbm, send_ref, rank_ref, owner_ref,
+                dose_v, owner_v, cell_v, offset_v, sems):
+    copies = [pltpu.make_async_copy(src, dst, sems.at[n]) for n, (src, dst) in enumerate(
+        ((owner_hbm, owner_v), (cell_hbm, cell_v), (offset_hbm, offset_v), (dose_hbm, dose_v)))]
+    for copy in copies:
+        copy.start()
     chunk = 256
     n_chunks = S_DEV // chunk
-    mine = owner == lax.broadcasted_iota(jnp.int32, (N_ROW, S_DEV), 0)
-    ones = jnp.where(mine, 1.0, 0.0)
-    stacked = jnp.concatenate([ones[:, c * chunk:(c + 1) * chunk] for c in range(n_chunks)], 0).astype(BF)
     rows_at = lax.broadcasted_iota(jnp.int32, (chunk, chunk), 0)
     cols_at = lax.broadcasted_iota(jnp.int32, (chunk, chunk), 1)
     before = jnp.where(rows_at < cols_at, 1.0, 0.0).astype(BF)
+    copies[0].wait()
+    owner = owner_v[...].astype(F32)
+    owner_ref[...] = owner
+    mine = equal_rows(owner, N_ROW)
+    ones = chosen(mine, jnp.ones((1, S_DEV), F32))
+    stacked = jnp.concatenate([ones[:, c * chunk:(c + 1) * chunk] for c in range(n_chunks)], 0)
     prefix = nn_dot(stacked, before)
     totals = nn_dot(stacked, jnp.ones((chunk, chunk), BF))
     base = jnp.zeros((N_ROW, chunk), F32)
     ranks = []
     for c in range(n_chunks):
         here = slice(c * N_ROW, (c + 1) * N_ROW)
-        inside = ones[:, c * chunk:(c + 1) * chunk]
+        inside = ones[:, c * chunk:(c + 1) * chunk].astype(F32)
         ranks.append(jnp.sum(inside * (prefix[here] + base), axis=0, keepdims=True))
         base = base + totals[here]
     rank = jnp.concatenate(ranks, 1)
     rank_ref[...] = rank
-    at_rank = jnp.where(rank == lax.broadcasted_iota(jnp.int32, (CAP, S_DEV), 0).astype(F32), 1.0, 0.0).astype(BF)
-    parts = [jnp.where(mine, part, 0.0).astype(BF) for part in split3(place) + split3(dose)]
+    at_rank = chosen(equal_rows(rank, CAP), jnp.ones((1, S_DEV), F32))
+    for copy in copies[1:]:
+        copy.wait()
+    place = (cell_v[...] * 256 + offset_v[...]).astype(F32)
+    dose = dose_v[...]
+    parts = [chosen(mine, part) for part in split3(place) + split3(dose)]
     packed = nt_dot(jnp.concatenate(parts, 0), at_rank)
     for which in range(2):
         p = packed[3 * which * N_ROW:3 * (which + 1) * N_ROW]
@@ -318,11 +346,11 @@
 
 
 def unpack_kernel(ret_ref, owner_ref, rank_ref, out_ref):
-    mine = owner_ref[...] == lax.broadcasted_iota(jnp.int32, (N_ROW, S_DEV), 0)
-    at_rank = jnp.where(rank_ref[...] == lax.broadcasted_iota(jnp.int32, (CAP, S_DEV), 0).astype(F32), 1.0, 0.0).astype(BF)
+    at_rank = chosen(equal_rows(rank_ref[...], CAP), jnp.ones((1, S_DEV), F32))
     parts = jnp.concatenate([p.astype(BF) for p in split3(ret_ref[:, 0, :])], 0)
     g = nn_dot(parts, at_rank)
     whole = g[:N_ROW] + g[N_ROW:2 * N_ROW] + g[2 * N_ROW:]
+    mine = owner_ref[...] == lax.broadcasted_iota(jnp.int32, (N_ROW, S_DEV), 0).astype(F32)
     out_ref[...] = jnp.sum(jnp.where(mine, whole, 0.0), axis=0, keepdims=True)
 
 
@@ -330,11 +358,11 @@
     return pl.BlockSpec(memory_space=pltpu.VMEM)
 
 
-def call(kernel, outs, n_in, scratch=()):
+def call(kernel, outs, n_in, scratch=(), space=pltpu.VMEM):
     return pl.pallas_call(
         kernel,
         out_shape=[jax.ShapeDtypeStruct(s, F32) for s in outs],
-        in_specs=[vmem()] * n_in,
+        in_specs=[pl.BlockSpec(memory_space=space)] * n_in,
         out_specs=[vmem() for _ in outs],
         scratch_shapes=list(scratch),
         compiler_params=pltpu.CompilerParams(vmem_limit_bytes=48 << 20),
@@ -349,12 +377,13 @@
 
 
 def per_device(shot_dose, shot_owner, shot_cell, shot_offset):
-    owner = shot_owner.reshape(1, S_DEV)
     ltaps = jnp.asarray(left_constant(3 * CY, NT * CY, CY))
     ltaps2 = jnp.asarray(left_constant(CY, 3 * CY, CY))
     rtaps = jnp.asarray(right_constant())
-    send, rank = call(pack_kernel, [(N_ROW, 1, 2 * NT * CAP), (1, S_DEV)], 4)(
-        shot_dose.reshape(1, S_DEV), owner, shot_cell.reshape(1, S_DEV), shot_offset.reshape(1, S_DEV)
+    row = (1, S_DEV)
+    rows = [pltpu.VMEM(row, F32)] + [pltpu.VMEM(row, jnp.int32)] * 3 + [pltpu.SemaphoreType.DMA((4,))]
+    send, rank, owner = call(pack_kernel, [(N_ROW, 1, 2 * NT * CAP), row, row], 4, rows, pltpu.HBM)(
+        *(pltpu.with_memory_space_constraint(v.reshape(row), pltpu.HBM) for v in (shot_dose, shot_owner, shot_cell, shot_offset))
     )
     recv = lax.all_to_all(send, "row", split_axis=0, concat_axis=0, tiled=True)
     edge = (3 * CY // 4, BLK)

time: 58.7 us -> 56.5 us (0.963)
  local copies, waits for them, and re-layouts: 2.8 us -> 0.01 us
  Pallas kernels: 11.2 us -> 12 us
    unnamed x16 -> x6, local copies, waits for them, and re-layouts: 2.8 us -> 0.01 us
    pallas_call x1, Pallas kernels: 0.75 us -> 1.54 us  [per_device(): call(pack_kernel, [(N_ROW, 1, 2 * NT * CAP), row, row], 4, rows, pltpu.HBM)]
where the time goes in v3:
time: 56.5 us; the launch traced here: 56.3 us
  blocking collectives  32.4 us (57%)
  Pallas kernels  12 us (21%)
  waiting for transfers between devices  8.09 us (14%)
  starting transfers between devices  3.07 us (5%)
  between operations  0.67 us (1%)
    all_to_all x1, blocking collectives, per_device(): recv = lax.all_to_all(send, 'row', split_axis=0, concat_axis=0, tiled=True)  20.8 us
    all_to_all x1, blocking collectives, per_device(): back = lax.all_to_all(final, 'row', split_axis=0, concat_axis=0, tiled=True)  11.7 us
    ppermute x2, waiting for transfers between devices, exchanged(): lax.ppermute(to_left, 'col', [((i + 1) % n, i) for i in range(n)])  6.61 us
    pallas_call x1, Pallas kernels, per_device(): call(second_kernel, [(N_ROW, CAP), (CY, CX), (CY, CX), edge, edge], 7, (p...  4.89 us
    pallas_call x1, Pallas kernels, per_device(): call(first_kernel, [(3 * CY, CX), (3 * CY, CX), edge, edge], 2)(recv, ltaps)  3.56 us
    ppermute x2, starting transfers between devices, exchanged(): lax.ppermute(to_right, 'col', [(i, (i + 1) % n) for i in range(n)])  2.59 us
    pallas_call x1, Pallas kernels, per_device(): call(pack_kernel, [(N_ROW, 1, 2 * NT * CAP), row, row], 4, rows, pltpu.HBM)  1.54 us
    ppermute x2, waiting for transfers between devices, exchanged(): lax.ppermute(to_right, 'col', [(i, (i + 1) % n) for i in range(n)])  1.48 us
  transfers between devices with their start and end apart: 4, of which 4 were waited for; matrix products, arithmetic and copies ran while one was open for 0% of the time, Pallas kernels for 0%

profile of v3, /device:TPU:7, one launch (start us, length us, event | category | flops | bytes accessed | tf_op | source)
XLA Modules:
  0.0 56.3 jit_solution(4149971396960149380)
XLA Ops:
  0.6 1.5 %shard_map.86 = (f32[32,1,1280]{2,1,0:T(1,128)S(1)}, f32[1,2048]{1,0:T(1,128)S(1)}, f32[1,2048]{1,0:T(1,128)S(1)}) custom-call(f32[1,2048]{1,0:T(1,128)} %bitcast.6, s32[1,2048]{1,0:T(1,128)} %bitcast.7, s32[1,2048]{1,0:T(1,128)} %bitcast.8, s32[1,2048]{1,0:T(1,128)} %bitcast.9), custom_call_target="tpu_custom_call" | custom-call | tf_op jit(solution)/shard_map/pallas_call | solution.py:385
  2.2 0.0 copy-start.1
  2.2 20.8 %all_to_all.10.recv_ref = f32[32,1,1280]{2,1,0:T(1,128)S(1)} all-to-all(f32[32,1,1280]{2,1,0:T(1,128)S(1)} %get-tuple-element.16), channel_id=1, replica_groups=mesh['row'=32,'col'=8] {'row'}, dimensions={0} | all-to-all | bytes 327680 | tf_op jit(solution)/shard_map/all_to_all | solution.py:388
  22.9 0.0 copy-done.1
  22.9 0.0 copy-start
  23.0 0.0 copy-start.2
  23.0 3.6 %shard_map.87 = (f32[96,512]{1,0:T(8,128)S(1)}, f32[96,512]{1,0:T(8,128)S(1)}, f32[24,128]{1,0:T(8,128)S(1)}, f32[24,128]{1,0:T(8,128)S(1)}) custom-call(f32[32,1,1280]{2,1,0:T(1,128)S(1)} %all_to_all.10.recv_ref, bf16[192,320]{1,0:T(8,128)(2,1)S(1)} %copy-done.1), custom_call_target="tpu_custom_call" | custom-call | tf_op jit(solution)/shard_map/pallas_call | solution.py:390
  26.5 2.5 %collective-permute-start = (f32[24,128]{1,0:T(8,128)S(1)}, f32[24,128]{1,0:T(8,128)S(1)}, u32[]{:S(2)}, u32[]{:S(2)}) collective-permute-start(f32[24,128]{1,0:T(8,128)S(1)} %get-tuple-element.19), channel_id=1, source_target_pairs={{0,1},{1,2},{2,3},{3,4},{4,5},{5,6},{6,7},{7,0},{8,9},{9,10},{10,1... | collective-permute-start | bytes 36872 | tf_op jit(solution)/shard_map/ppermute | solution.py:374
  29.1 0.0 collective-permute-start.1
  29.1 0.8 %collective-permute-done.from_left_ref = f32[24,128]{1,0:T(8,128)S(1)} collective-permute-done((f32[24,128]{1,0:T(8,128)S(1)}, f32[24,128]{1,0:T(8,128)S(1)}, u32[]{:S(2)}, u32[]{:S(2)}) %collective-permute-start) | collective-permute-done | bytes 12320 | tf_op jit(solution)/shard_map/ppermute | solution.py:374
  29.9 3.5 %collective-permute-done.1.from_right_ref = f32[24,128]{1,0:T(8,128)S(1)} collective-permute-done((f32[24,128]{1,0:T(8,128)S(1)}, f32[24,128]{1,0:T(8,128)S(1)}, u32[]{:S(2)}, u32[]{:S(2)}) %collective-permute-start.1) | collective-permute-done | bytes 12320 | tf_op jit(solution)/shard_map/ppermute | solution.py:375
  33.4 0.0 copy-done
  33.4 0.0 copy-done.2
  33.4 4.9 %shard_map.88 = (f32[32,128]{1,0:T(8,128)S(1)}, f32[32,512]{1,0:T(8,128)S(1)}, f32[32,512]{1,0:T(8,128)S(1)}, f32[8,128]{1,0:T(8,128)S(1)}, f32[8,128]{1,0:T(8,128)S(1)}) custom-call(f32[32,1,1280]{2,1,0:T(1,128)S(1)} %all_to_all.10.recv_ref, f32[96,512]{1,0:T(8,128)S(1)} %get-tuple-element.17.along_ref, f32[96,512]{1,0:T(8,128)S(1)} %get-tuple-element.18.density_ref, ...), custom_call_target="tpu_custom_call" | custom-call | tf_op jit(solution)/shard_map/pallas_call | solution.py:393
  38.3 0.1 collective-permute-start.2
  38.3 0.5 collective-permute-start.3
  38.8 0.7 %collective-permute-done.2.from_left_ref = f32[8,128]{1,0:T(8,128)S(1)} collective-permute-done((f32[8,128]{1,0:T(8,128)S(1)}, f32[8,128]{1,0:T(8,128)S(1)}, u32[]{:S(2)}, u32[]{:S(2)}) %collective-permute-start.2) | collective-permute-done | bytes 4128 | tf_op jit(solution)/shard_map/ppermute | solution.py:374
  39.5 3.1 %collective-permute-done.3.from_right_ref = f32[8,128]{1,0:T(8,128)S(1)} collective-permute-done((f32[8,128]{1,0:T(8,128)S(1)}, f32[8,128]{1,0:T(8,128)S(1)}, u32[]{:S(2)}, u32[]{:S(2)}) %collective-permute-start.3) | collective-permute-done | bytes 4128 | tf_op jit(solution)/shard_map/ppermute | solution.py:375
  42.6 1.1 %shard_map.89 = (f32[32,512]{1,0:T(8,128)}, f32[32,1,128]{2,1,0:T(1,128)S(1)}) custom-call(f32[32,1,1280]{2,1,0:T(1,128)S(1)} %all_to_all.10.recv_ref, f32[32,128]{1,0:T(8,128)S(1)} %get-tuple-element.21.dose_ref, f32[32,512]{1,0:T(8,128)S(1)} %get-tuple-element.22.along_ref, f32[32,512]{1,0:T(8,128)S(1)} %get-tuple-element.23.density_ref, ...), custom_call_target="tpu_custom_call" | custom-call | tf_op jit(solution)/shard_map/pallas_call | solution.py:397
  43.7 11.7 %all_to_all.11.ret_ref = f32[32,1,128]{2,1,0:T(1,128)S(1)} all-to-all(f32[32,1,128]{2,1,0:T(1,128)S(1)} %get-tuple-element.26), channel_id=1, replica_groups=mesh['row'=32,'col'=8] {'row'}, dimensions={0} | all-to-all | bytes 32768 | tf_op jit(solution)/shard_map/all_to_all | solution.py:400
  55.4 0.9 %shard_map.90 = f32[1,2048]{1,0:T(1,128)} custom-call(f32[32,1,128]{2,1,0:T(1,128)S(1)} %all_to_all.11.ret_ref, f32[1,2048]{1,0:T(1,128)S(1)} %get-tuple-element.27.owner_ref, f32[1,2048]{1,0:T(1,128)S(1)} %get-tuple-element.28.rank_ref), custom_call_target="tpu_custom_call" | custom-call | tf_op jit(solution)/shard_map/pallas_call | solution.py:401
Async XLA Ops:
  2.2 20.8 %copy-start.1 = (bf16[192,320]{1,0:T(8,128)(2,1)S(1)}, bf16[192,320]{1,0:T(8,128)(2,1)}, u32[]{:S(2)}) copy-start(bf16[192,320]{1,0:T(8,128)(2,1)} %constant.6.clone.ltaps_ref) | copy-start | bytes 368644
  22.9 10.4 %copy-start = (bf16[384,256]{1,0:T(8,128)(2,1)S(1)}, bf16[384,256]{1,0:T(8,128)(2,1)}, u32[]{:S(2)}) copy-start(bf16[384,256]{1,0:T(8,128)(2,1)} %constant.8.clone.rtaps_ref) | copy-start | bytes 589828
  23.0 10.4 %copy-start.2 = (bf16[64,192]{1,0:T(8,128)(2,1)S(1)}, bf16[64,192]{1,0:T(8,128)(2,1)}, u32[]{:S(2)}) copy-start(bf16[64,192]{1,0:T(8,128)(2,1)} %constant.7.clone.ltaps_ref) | copy-start | bytes 73732
  26.5 3.4 %collective-permute-start = (f32[24,128]{1,0:T(8,128)S(1)}, f32[24,128]{1,0:T(8,128)S(1)}, u32[]{:S(2)}, u32[]{:S(2)}) collective-permute-start(f32[24,128]{1,0:T(8,128)S(1)} %get-tuple-element.19), channel_id=1, source_target_pairs={{0,1},{1,2},{2,3},{3,4},{4,5},{5,6},{6,7},{7,0},{8,9},{9,10},{10,1... | collective-permute-start | bytes 36872 | tf_op jit(solution)/shard_map/ppermute | solution.py:374
  29.1 4.3 %collective-permute-start.1 = (f32[24,128]{1,0:T(8,128)S(1)}, f32[24,128]{1,0:T(8,128)S(1)}, u32[]{:S(2)}, u32[]{:S(2)}) collective-permute-start(f32[24,128]{1,0:T(8,128)S(1)} %get-tuple-element.20), channel_id=1, source_target_pairs={{1,0},{2,1},{3,2},{4,3},{5,4},{6,5},{7,6},{0,7},{9,8},{10,9},{11,1... | collective-permute-start | bytes 36872 | tf_op jit(solution)/shard_map/ppermute | solution.py:375
  38.3 1.2 %collective-permute-start.2 = (f32[8,128]{1,0:T(8,128)S(1)}, f32[8,128]{1,0:T(8,128)S(1)}, u32[]{:S(2)}, u32[]{:S(2)}) collective-permute-start(f32[8,128]{1,0:T(8,128)S(1)} %get-tuple-element.24), channel_id=1, source_target_pairs={{0,1},{1,2},{2,3},{3,4},{4,5},{5,6},{6,7},{7,0},{8,9},{9,10},{10,1... | collective-permute-start | bytes 12296 | tf_op jit(solution)/shard_map/ppermute | solution.py:374
  38.3 4.2 %collective-permute-start.3 = (f32[8,128]{1,0:T(8,128)S(1)}, f32[8,128]{1,0:T(8,128)S(1)}, u32[]{:S(2)}, u32[]{:S(2)}) collective-permute-start(f32[8,128]{1,0:T(8,128)S(1)} %get-tuple-element.25), channel_id=1, source_target_pairs={{1,0},{2,1},{3,2},{4,3},{5,4},{6,5},{7,6},{0,7},{9,8},{10,9},{11,1... | collective-permute-start | bytes 12296 | tf_op jit(solution)/shard_map/ppermute | solution.py:375

commit v4 on v3

--- a/solution.py
+++ b/solution.py
@@ -19,6 +19,7 @@
 NB = CX // BLK
 XR = BLK + 16
 SLOTS = N_ROW * CAP
+GROUP = 8
 SUB16 = 16
 BF = jnp.bfloat16
 F32 = jnp.float32
@@ -159,8 +160,8 @@
                 y0w=1.0 - off_y, y1w=off_y, x0=1.0 - off_x, x1=off_x)
 
 
-def pair_columns(shot):
-    return lambda i: jnp.concatenate([column_chunk(shot, i), column_chunk(shot, i + 1)], 1)
+def pair_columns(shot, i):
+    return jnp.concatenate([column_chunk(shot, i), column_chunk(shot, i + 1)], 1)
 
 
 def over_rows(v, i):
@@ -182,10 +183,10 @@
     return jnp.concatenate(out, 0)
 
 
-def row_chunk(shot, dosed, i):
+def row_chunk(shot, dosed, i, at_dosed):
     first, second = over_rows(shot["y"], i), over_rows(shot["y1"], i)
     block = over_rows(shot["block"], i)
-    values = [over_rows(v, i) for v in dosed]
+    values = [over_rows(v, at_dosed) for v in dosed]
     none = jnp.zeros_like(first)
     parts = [[], []]
     for k in range(CY // SUB16):
@@ -198,19 +199,18 @@
     return jnp.concatenate([jnp.where(inside[h], v, none) for part in parts for h in range(NB) for v in part], 0)
 
 
-def dosed_weights(shot, dose):
-    hi0, lo0 = split2(shot["y0w"] * dose)
-    hi1, lo1 = split2(shot["y1w"] * dose)
+def dosed_weights(shot, dose, sources=slice(None)):
+    hi0, lo0 = split2(shot["y0w"][sources] * dose)
+    hi1, lo1 = split2(shot["y1w"][sources] * dose)
     return [v.astype(F32) for v in (hi0, hi1, lo0, lo1)]
 
 
-def tile_density(shot, dose, columns):
-    dosed = dosed_weights(shot, dose)
-    both = None
-    for i in range(0, N_ROW, 2):
-        a = jnp.concatenate([row_chunk(shot, dosed, i), row_chunk(shot, dosed, i + 1)], 1)
-        one = nt_dot(a, columns(i))
-        both = one if both is None else both + one
+def density_pair(shot, dosed, first, i, columns):
+    a = jnp.concatenate([row_chunk(shot, dosed, j, j - first) for j in (i, i + 1)], 1)
+    return nt_dot(a, columns)
+
+
+def assembled(both):
     d = both[:BLK] + both[BLK:]
     blocks = [d[:CY, :BLK]]
     for h in range(1, NB):
@@ -218,6 +218,18 @@
         over = jnp.concatenate([over, jnp.zeros((CY, BLK - XR + BLK), F32)], 1)
         blocks.append(d[h * CY:(h + 1) * CY, :BLK] + over)
     return jnp.concatenate(blocks, 1)
+
+
+def added(total, one):
+    return one if total is None else total + one
+
+
+def tile_density(shot, dose):
+    dosed = dosed_weights(shot, dose)
+    both = None
+    for i in range(0, N_ROW, 2):
+        both = added(both, density_pair(shot, dosed, 0, i, pair_columns(shot, i)))
+    return assembled(both)
 
 
 def packed_edge(block, lane0):
@@ -258,7 +270,7 @@
     return jnp.concatenate([out[h * rows:(h + 1) * rows] for h in range(NB)], 1)
 
 
-def gathered(total, shot, b_ref):
+def gather_table(total):
     pieces = []
     for h in range(NB):
         inside = total[:, h * BLK:(h + 1) * BLK]
@@ -267,26 +279,23 @@
         else:
             after = jnp.zeros((CY, XR - BLK), F32)
         pieces.append(jnp.concatenate([inside, after], 1))
-    hi, lo = split2(jnp.concatenate(pieces, 0))
-    table = jnp.concatenate([hi, lo], 0)
+    return jnp.concatenate(split2(jnp.concatenate(pieces, 0)), 0)
+
+
+def gather_pair(table, shot, i, columns):
+    both = nn_dot(table, columns)
     at = lax.broadcasted_iota(jnp.int32, (CY, CAP), 0).astype(F32)
     rows = []
-    for i in range(0, N_ROW, 2):
-        columns = pair_columns(shot)(i)
-        if b_ref is not None:
-            b_ref[:, i * CAP:(i + 2) * CAP] = columns
-        both = nn_dot(table, columns)
-        for j in range(2):
-            here = slice(j * CAP, (j + 1) * CAP)
-            g = both[:BLK, here] + both[BLK:, here]
-            block = shot["block"][i + j:i + j + 1]
-            mine = g[:CY]
-            for h in range(1, NB):
-                mine = jnp.where(block == float(h), g[h * CY:(h + 1) * CY], mine)
-            y, y1 = shot["y"][i + j:i + j + 1], shot["y1"][i + j:i + j + 1]
-            w = jnp.where(at == y, shot["y0w"][i + j:i + j + 1], jnp.where(at == y1, shot["y1w"][i + j:i + j + 1], 0.0))
-            rows.append(jnp.sum(w * mine, axis=0, keepdims=True))
-    return jnp.concatenate(rows, 0)
+    for j in range(2):
+        here = slice(j * CAP, (j + 1) * CAP)
+        g = both[:BLK, here] + both[BLK:, here]
+        block, y, y1, w0, w1 = (shot[name][i + j:i + j + 1] for name in ("block", "y", "y1", "y0w", "y1w"))
+        mine = g[:CY]
+        for h in range(1, NB):
+            mine = jnp.where(block == float(h), g[h * CY:(h + 1) * CY], mine)
+        w = jnp.where(at == y, w0, jnp.where(at == y1, w1, 0.0))
+        rows.append(jnp.sum(w * mine, axis=0, keepdims=True))
+    return rows
 
 
 def corrected(dose, exposure):
@@ -303,7 +312,7 @@
     for t in range(NT):
         place, dose = slots(recv_ref, t)
         shot = decoded(place)
-        tiles.append(tile_density(shot, dose, pair_columns(shot)))
+        tiles.append(tile_density(shot, dose))
     density_ref[...] = jnp.concatenate(tiles[1:NT - 1], 0)
     along = blurred_y(jnp.concatenate(tiles, 0), ltaps_ref)
     along_ref[...] = along
@@ -321,15 +330,31 @@
 def second_kernel(recv_ref, along_ref, density_ref, from_left_ref, from_right_ref, rtaps_ref, ltaps_ref,
                   dose_ref, along2_ref, density2_ref, to_left_ref, to_right_ref, b_ref):
     total = density_ref[...] + BACKSCATTER * field_of(along_ref, from_left_ref, from_right_ref, rtaps_ref)
-    tiles = []
-    for n in range(NT - 2):
-        place, dose = slots(recv_ref, n + 1)
-        shot = decoded(place)
-        exposure = gathered(total[n * CY:(n + 1) * CY], shot, b_ref)
-        dose = corrected(dose, exposure)
-        if n + 1 == REACH:
-            dose_ref[...] = dose
-        tiles.append(tile_density(shot, dose, lambda i: b_ref[:, i * CAP:(i + 2) * CAP]))
+    places = [slots(recv_ref, n + 1) for n in range(NT - 2)]
+    shots = [decoded(place) for place, _ in places]
+    tables = [gather_table(total[n * CY:(n + 1) * CY]) for n in range(NT - 2)]
+    densities = [None] * (NT - 2)
+    groups = [(n, first) for n in range(NT - 2) for first in range(0, N_ROW, GROUP)]
+    dosed = None
+    for step in range(len(groups) + 1):
+        rows = []
+        for j in range(0, GROUP, 2):
+            if step < len(groups):
+                n, first = groups[step]
+                columns = pair_columns(shots[n], first + j)
+                b_ref[n, :, (first + j) * CAP:(first + j + 2) * CAP] = columns
+                rows += gather_pair(tables[n], shots[n], first + j, columns)
+            if step > 0:
+                m, start = groups[step - 1]
+                columns = b_ref[m, :, (start + j) * CAP:(start + j + 2) * CAP]
+                densities[m] = added(densities[m], density_pair(shots[m], dosed, start, start + j, columns))
+        if rows:
+            sources = slice(first, first + GROUP)
+            dose = corrected(places[n][1][sources], jnp.concatenate(rows, 0))
+            if n + 1 == REACH:
+                dose_ref[sources, :] = dose
+            dosed = dosed_weights(shots[n], dose, sources)
+    tiles = [assembled(both) for both in densities]
     density2_ref[...] = tiles[1]
     along = blurred_y(jnp.concatenate(tiles, 0), ltaps_ref)
     along2_ref[...] = along
@@ -337,12 +362,19 @@
     to_right_ref[...] = packed_edge(along[:, CX - BLK:], BLK - 32)
 
 
-def third_kernel(recv_ref, dose_ref, along_ref, density_ref, from_left_ref, from_right_ref, rtaps_ref, field_ref, final_ref):
+def third_kernel(recv_ref, dose_ref, along_ref, density_ref, from_left_ref, from_right_ref, rtaps_ref, field_hbm, final_ref,
+                 field_ref, sem):
     field = field_of(along_ref, from_left_ref, from_right_ref, rtaps_ref)
     field_ref[...] = field
-    place, _ = slots(recv_ref, REACH)
-    exposure = gathered(density_ref[...] + BACKSCATTER * field, decoded(place), None)
-    final_ref[:, 0, :] = corrected(dose_ref[...], exposure)
+    copy = pltpu.make_async_copy(field_ref, field_hbm, sem)
+    copy.start()
+    shot = decoded(slots(recv_ref, REACH)[0])
+    table = gather_table(density_ref[...] + BACKSCATTER * field)
+    rows = []
+    for i in range(0, N_ROW, 2):
+        rows += gather_pair(table, shot, i, pair_columns(shot, i))
+    final_ref[:, 0, :] = corrected(dose_ref[...], jnp.concatenate(rows, 0))
+    copy.wait()
 
 
 def unpack_kernel(ret_ref, owner_ref, rank_ref, out_ref):
@@ -354,16 +386,12 @@
     out_ref[...] = jnp.sum(jnp.where(mine, whole, 0.0), axis=0, keepdims=True)
 
 
-def vmem():
-    return pl.BlockSpec(memory_space=pltpu.VMEM)
-
-
-def call(kernel, outs, n_in, scratch=(), space=pltpu.VMEM):
+def call(kernel, outs, n_in, scratch=(), space=pltpu.VMEM, out_spaces=None):
     return pl.pallas_call(
         kernel,
         out_shape=[jax.ShapeDtypeStruct(s, F32) for s in outs],
         in_specs=[pl.BlockSpec(memory_space=space)] * n_in,
-        out_specs=[vmem() for _ in outs],
+        out_specs=[pl.BlockSpec(memory_space=s) for s in out_spaces or [pltpu.VMEM] * len(outs)],
         scratch_shapes=list(scratch),
         compiler_params=pltpu.CompilerParams(vmem_limit_bytes=48 << 20),
     )
@@ -391,10 +419,13 @@
     from_left, from_right = exchanged(to_left, to_right)
     edge = (CY // 4, BLK)
     dose, along, density, to_left, to_right = call(
-        second_kernel, [(N_ROW, CAP), (CY, CX), (CY, CX), edge, edge], 7, (pltpu.VMEM((XR, SLOTS), BF),)
+        second_kernel, [(N_ROW, CAP), (CY, CX), (CY, CX), edge, edge], 7, (pltpu.VMEM((NT - 2, XR, SLOTS), BF),)
     )(recv, along, density, from_left, from_right, rtaps, ltaps2)
     from_left, from_right = exchanged(to_left, to_right)
-    field, final = call(third_kernel, [(CY, CX), (N_ROW, 1, CAP)], 7)(
+    field, final = call(
+        third_kernel, [(CY, CX), (N_ROW, 1, CAP)], 7, (pltpu.VMEM((CY, CX), F32), pltpu.SemaphoreType.DMA),
+        out_spaces=[pltpu.HBM, pltpu.VMEM],
+    )(
         recv, dose, along, density, from_left, from_right, rtaps
     )
     back = lax.all_to_all(final, "row", split_axis=0, concat_axis=0, tiled=True)

time: 56.5 us -> 56.1 us (level)
  no operation moved by 1% of the time
where the time goes in v4:
time: 56.1 us; the launch traced here: 55.9 us
  blocking collectives  32.4 us (58%)
  Pallas kernels  11.7 us (21%)
  waiting for transfers between devices  8.09 us (14%)
  starting transfers between devices  3.07 us (5%)
  between operations  0.67 us (1%)
    all_to_all x1, blocking collectives, per_device(): recv = lax.all_to_all(send, 'row', split_axis=0, concat_axis=0, tiled=True)  20.8 us
    all_to_all x1, blocking collectives, per_device(): back = lax.all_to_all(final, 'row', split_axis=0, concat_axis=0, tiled=True)  11.7 us
    ppermute x2, waiting for transfers between devices, exchanged(): lax.ppermute(to_left, 'col', [((i + 1) % n, i) for i in range(n)])  6.6 us
    pallas_call x1, Pallas kernels, per_device(): call(second_kernel, [(N_ROW, CAP), (CY, CX), (CY, CX), edge, edge], 7, (p...  4.52 us
    pallas_call x1, Pallas kernels, per_device(): call(first_kernel, [(3 * CY, CX), (3 * CY, CX), edge, edge], 2)(recv, ltaps)  3.56 us
    ppermute x2, starting transfers between devices, exchanged(): lax.ppermute(to_right, 'col', [(i, (i + 1) % n) for i in range(n)])  2.59 us
    pallas_call x1, Pallas kernels, per_device(): call(pack_kernel, [(N_ROW, 1, 2 * NT * CAP), row, row], 4, rows, pltpu.HBM)  1.54 us
    ppermute x2, waiting for transfers between devices, exchanged(): lax.ppermute(to_right, 'col', [(i, (i + 1) % n) for i in range(n)])  1.48 us
  transfers between devices with their start and end apart: 4, of which 4 were waited for; matrix products, arithmetic and copies ran while one was open for 0% of the time, Pallas kernels for 0%

profile of v4, /device:TPU:7, one launch (start us, length us, event | category | flops | bytes accessed | tf_op | source)
XLA Modules:
  0.0 55.9 jit_solution(7166665926189346599)
XLA Ops:
  0.6 1.5 %shard_map.86 = (f32[32,1,1280]{2,1,0:T(1,128)S(1)}, f32[1,2048]{1,0:T(1,128)S(1)}, f32[1,2048]{1,0:T(1,128)S(1)}) custom-call(f32[1,2048]{1,0:T(1,128)} %bitcast.6, s32[1,2048]{1,0:T(1,128)} %bitcast.7, s32[1,2048]{1,0:T(1,128)} %bitcast.8, s32[1,2048]{1,0:T(1,128)} %bitcast.9), custom_call_target="tpu_custom_call" | custom-call | tf_op jit(solution)/shard_map/pallas_call | solution.py:413
  2.2 0.0 copy-start.1
  2.2 20.8 %all_to_all.10.recv_ref = f32[32,1,1280]{2,1,0:T(1,128)S(1)} all-to-all(f32[32,1,1280]{2,1,0:T(1,128)S(1)} %get-tuple-element.16), channel_id=1, replica_groups=mesh['row'=32,'col'=8] {'row'}, dimensions={0} | all-to-all | bytes 327680 | tf_op jit(solution)/shard_map/all_to_all | solution.py:416
  22.9 0.0 copy-done.1
  22.9 0.0 copy-start
  23.0 0.0 copy-start.2
  23.0 3.6 %shard_map.87 = (f32[96,512]{1,0:T(8,128)S(1)}, f32[96,512]{1,0:T(8,128)S(1)}, f32[24,128]{1,0:T(8,128)S(1)}, f32[24,128]{1,0:T(8,128)S(1)}) custom-call(f32[32,1,1280]{2,1,0:T(1,128)S(1)} %all_to_all.10.recv_ref, bf16[192,320]{1,0:T(8,128)(2,1)S(1)} %copy-done.1), custom_call_target="tpu_custom_call" | custom-call | tf_op jit(solution)/shard_map/pallas_call | solution.py:418
  26.5 2.5 %collective-permute-start = (f32[24,128]{1,0:T(8,128)S(1)}, f32[24,128]{1,0:T(8,128)S(1)}, u32[]{:S(2)}, u32[]{:S(2)}) collective-permute-start(f32[24,128]{1,0:T(8,128)S(1)} %get-tuple-element.19), channel_id=1, source_target_pairs={{0,1},{1,2},{2,3},{3,4},{4,5},{5,6},{6,7},{7,0},{8,9},{9,10},{10,1... | collective-permute-start | bytes 36872 | tf_op jit(solution)/shard_map/ppermute | solution.py:402
  29.1 0.0 collective-permute-start.1
  29.1 0.8 %collective-permute-done.from_left_ref = f32[24,128]{1,0:T(8,128)S(1)} collective-permute-done((f32[24,128]{1,0:T(8,128)S(1)}, f32[24,128]{1,0:T(8,128)S(1)}, u32[]{:S(2)}, u32[]{:S(2)}) %collective-permute-start) | collective-permute-done | bytes 12320 | tf_op jit(solution)/shard_map/ppermute | solution.py:402
  29.9 3.5 %collective-permute-done.1.from_right_ref = f32[24,128]{1,0:T(8,128)S(1)} collective-permute-done((f32[24,128]{1,0:T(8,128)S(1)}, f32[24,128]{1,0:T(8,128)S(1)}, u32[]{:S(2)}, u32[]{:S(2)}) %collective-permute-start.1) | collective-permute-done | bytes 12320 | tf_op jit(solution)/shard_map/ppermute | solution.py:403
  33.4 0.0 copy-done
  33.4 0.0 copy-done.2
  33.4 4.5 %shard_map.88 = (f32[32,128]{1,0:T(8,128)S(1)}, f32[32,512]{1,0:T(8,128)S(1)}, f32[32,512]{1,0:T(8,128)S(1)}, f32[8,128]{1,0:T(8,128)S(1)}, f32[8,128]{1,0:T(8,128)S(1)}) custom-call(f32[32,1,1280]{2,1,0:T(1,128)S(1)} %all_to_all.10.recv_ref, f32[96,512]{1,0:T(8,128)S(1)} %get-tuple-element.17.along_ref, f32[96,512]{1,0:T(8,128)S(1)} %get-tuple-element.18.density_ref, ...), custom_call_target="tpu_custom_call" | custom-call | tf_op jit(solution)/shard_map/pallas_call | solution.py:421
  37.9 0.1 collective-permute-start.2
  38.0 0.5 collective-permute-start.3
  38.4 0.7 %collective-permute-done.2.from_left_ref = f32[8,128]{1,0:T(8,128)S(1)} collective-permute-done((f32[8,128]{1,0:T(8,128)S(1)}, f32[8,128]{1,0:T(8,128)S(1)}, u32[]{:S(2)}, u32[]{:S(2)}) %collective-permute-start.2) | collective-permute-done | bytes 4128 | tf_op jit(solution)/shard_map/ppermute | solution.py:402
  39.1 3.1 %collective-permute-done.3.from_right_ref = f32[8,128]{1,0:T(8,128)S(1)} collective-permute-done((f32[8,128]{1,0:T(8,128)S(1)}, f32[8,128]{1,0:T(8,128)S(1)}, u32[]{:S(2)}, u32[]{:S(2)}) %collective-permute-start.3) | collective-permute-done | bytes 4128 | tf_op jit(solution)/shard_map/ppermute | solution.py:403
  42.2 1.1 %shard_map.89 = (f32[32,512]{1,0:T(8,128)}, f32[32,1,128]{2,1,0:T(1,128)S(1)}) custom-call(f32[32,1,1280]{2,1,0:T(1,128)S(1)} %all_to_all.10.recv_ref, f32[32,128]{1,0:T(8,128)S(1)} %get-tuple-element.21.dose_ref, f32[32,512]{1,0:T(8,128)S(1)} %get-tuple-element.22.along_ref, f32[32,512]{1,0:T(8,128)S(1)} %get-tuple-element.23.density_ref, ...), custom_call_target="tpu_custom_call" | custom-call | tf_op jit(solution)/shard_map/pallas_call | solution.py:425
  43.3 11.7 %all_to_all.11.ret_ref = f32[32,1,128]{2,1,0:T(1,128)S(1)} all-to-all(f32[32,1,128]{2,1,0:T(1,128)S(1)} %get-tuple-element.26), channel_id=1, replica_groups=mesh['row'=32,'col'=8] {'row'}, dimensions={0} | all-to-all | bytes 32768 | tf_op jit(solution)/shard_map/all_to_all | solution.py:431
  55.0 0.9 %shard_map.90 = f32[1,2048]{1,0:T(1,128)} custom-call(f32[32,1,128]{2,1,0:T(1,128)S(1)} %all_to_all.11.ret_ref, f32[1,2048]{1,0:T(1,128)S(1)} %get-tuple-element.27.owner_ref, f32[1,2048]{1,0:T(1,128)S(1)} %get-tuple-element.28.rank_ref), custom_call_target="tpu_custom_call" | custom-call | tf_op jit(solution)/shard_map/pallas_call | solution.py:432
Async XLA Ops:
  2.2 20.8 %copy-start.1 = (bf16[192,320]{1,0:T(8,128)(2,1)S(1)}, bf16[192,320]{1,0:T(8,128)(2,1)}, u32[]{:S(2)}) copy-start(bf16[192,320]{1,0:T(8,128)(2,1)} %constant.6.clone.ltaps_ref) | copy-start | bytes 368644
  22.9 10.4 %copy-start = (bf16[384,256]{1,0:T(8,128)(2,1)S(1)}, bf16[384,256]{1,0:T(8,128)(2,1)}, u32[]{:S(2)}) copy-start(bf16[384,256]{1,0:T(8,128)(2,1)} %constant.8.clone.rtaps_ref) | copy-start | bytes 589828
  23.0 10.4 %copy-start.2 = (bf16[64,192]{1,0:T(8,128)(2,1)S(1)}, bf16[64,192]{1,0:T(8,128)(2,1)}, u32[]{:S(2)}) copy-start(bf16[64,192]{1,0:T(8,128)(2,1)} %constant.7.clone.ltaps_ref) | copy-start | bytes 73732
  26.5 3.4 %collective-permute-start = (f32[24,128]{1,0:T(8,128)S(1)}, f32[24,128]{1,0:T(8,128)S(1)}, u32[]{:S(2)}, u32[]{:S(2)}) collective-permute-start(f32[24,128]{1,0:T(8,128)S(1)} %get-tuple-element.19), channel_id=1, source_target_pairs={{0,1},{1,2},{2,3},{3,4},{4,5},{5,6},{6,7},{7,0},{8,9},{9,10},{10,1... | collective-permute-start | bytes 36872 | tf_op jit(solution)/shard_map/ppermute | solution.py:402
  29.1 4.3 %collective-permute-start.1 = (f32[24,128]{1,0:T(8,128)S(1)}, f32[24,128]{1,0:T(8,128)S(1)}, u32[]{:S(2)}, u32[]{:S(2)}) collective-permute-start(f32[24,128]{1,0:T(8,128)S(1)} %get-tuple-element.20), channel_id=1, source_target_pairs={{1,0},{2,1},{3,2},{4,3},{5,4},{6,5},{7,6},{0,7},{9,8},{10,9},{11,1... | collective-permute-start | bytes 36872 | tf_op jit(solution)/shard_map/ppermute | solution.py:403
  37.9 1.2 %collective-permute-start.2 = (f32[8,128]{1,0:T(8,128)S(1)}, f32[8,128]{1,0:T(8,128)S(1)}, u32[]{:S(2)}, u32[]{:S(2)}) collective-permute-start(f32[8,128]{1,0:T(8,128)S(1)} %get-tuple-element.24), channel_id=1, source_target_pairs={{0,1},{1,2},{2,3},{3,4},{4,5},{5,6},{6,7},{7,0},{8,9},{9,10},{10,1... | collective-permute-start | bytes 12296 | tf_op jit(solution)/shard_map/ppermute | solution.py:402
  38.0 4.2 %collective-permute-start.3 = (f32[8,128]{1,0:T(8,128)S(1)}, f32[8,128]{1,0:T(8,128)S(1)}, u32[]{:S(2)}, u32[]{:S(2)}) collective-permute-start(f32[8,128]{1,0:T(8,128)S(1)} %get-tuple-element.25), channel_id=1, source_target_pairs={{1,0},{2,1},{3,2},{4,3},{5,4},{6,5},{7,6},{0,7},{9,8},{10,9},{11,1... | collective-permute-start | bytes 12296 | tf_op jit(solution)/shard_map/ppermute | solution.py:403

commit v5 on v4

--- a/solution.py
+++ b/solution.py
@@ -259,15 +259,26 @@
     return both[:rows] + both[rows:]
 
 
-def blurred_x(along_y, left, right, taps_ref):
-    wide = jnp.concatenate([left, along_y, right], 1)
+def edge_products(stacked, taps):
+    both = nn_dot(jnp.concatenate(split2(stacked), 0), taps)
+    rows = stacked.shape[0]
+    both = both[:rows] + both[rows:]
+    return both[:, :BLK] + both[:, BLK:]
+
+
+def blurred_inside(along_y, taps_ref):
+    none = jnp.zeros((along_y.shape[0], BLK), F32)
+    wide = jnp.concatenate([none, along_y, none], 1)
     rows = along_y.shape[0]
-    stacked = jnp.concatenate([wide[:, h * BLK:(h + 3) * BLK] for h in range(NB)], 0)
-    hi, lo = split2(stacked)
-    both = nn_dot(jnp.concatenate([hi, lo], 0), taps_ref[...])
-    both = both[:NB * rows] + both[NB * rows:]
-    out = both[:, :BLK] + both[:, BLK:]
+    out = edge_products(jnp.concatenate([wide[:, h * BLK:(h + 3) * BLK] for h in range(NB)], 0), taps_ref[...])
     return jnp.concatenate([out[h * rows:(h + 1) * rows] for h in range(NB)], 1)
+
+
+def blurred_sides(from_left_ref, from_right_ref, taps_ref):
+    col = lax.axis_index("col")
+    left = unpacked_edge(jnp.where(col > 0, from_left_ref[...], 0.0), BLK - 32)
+    right = unpacked_edge(jnp.where(col < N_COL - 1, from_right_ref[...], 0.0), 0)
+    return edge_products(left, taps_ref[:BLK]), edge_products(right, taps_ref[2 * BLK:])
 
 
 def gather_table(total):
@@ -320,16 +331,19 @@
     to_right_ref[...] = packed_edge(along[:, CX - BLK:], BLK - 32)
 
 
-def field_of(along_ref, from_left_ref, from_right_ref, rtaps_ref):
-    col = lax.axis_index("col")
-    left = unpacked_edge(jnp.where(col > 0, from_left_ref[...], 0.0), BLK - 32)
-    right = unpacked_edge(jnp.where(col < N_COL - 1, from_right_ref[...], 0.0), 0)
-    return blurred_x(along_ref[...], left, right, rtaps_ref)
-
-
-def second_kernel(recv_ref, along_ref, density_ref, from_left_ref, from_right_ref, rtaps_ref, ltaps_ref,
+def inside_kernel(along_ref, rtaps_ref, field_ref):
+    field_ref[...] = blurred_inside(along_ref[...], rtaps_ref)
+
+
+def full_field(inside_ref, from_left_ref, from_right_ref, rtaps_ref):
+    left, right = blurred_sides(from_left_ref, from_right_ref, rtaps_ref)
+    return jnp.concatenate(
+        [inside_ref[:, :BLK] + left, inside_ref[:, BLK:CX - BLK], inside_ref[:, CX - BLK:] + right], 1)
+
+
+def second_kernel(recv_ref, inside_ref, density_ref, from_left_ref, from_right_ref, rtaps_ref, ltaps_ref,
                   dose_ref, along2_ref, density2_ref, to_left_ref, to_right_ref, b_ref):
-    total = density_ref[...] + BACKSCATTER * field_of(along_ref, from_left_ref, from_right_ref, rtaps_ref)
+    total = density_ref[...] + BACKSCATTER * full_field(inside_ref, from_left_ref, from_right_ref, rtaps_ref)
     places = [slots(recv_ref, n + 1) for n in range(NT - 2)]
     shots = [decoded(place) for place, _ in places]
     tables = [gather_table(total[n * CY:(n + 1) * CY]) for n in range(NT - 2)]
@@ -362,9 +376,9 @@
     to_right_ref[...] = packed_edge(along[:, CX - BLK:], BLK - 32)
 
 
-def third_kernel(recv_ref, dose_ref, along_ref, density_ref, from_left_ref, from_right_ref, rtaps_ref, field_hbm, final_ref,
+def third_kernel(recv_ref, dose_ref, inside_ref, density_ref, from_left_ref, from_right_ref, rtaps_ref, field_hbm, final_ref,
                  field_ref, sem):
-    field = field_of(along_ref, from_left_ref, from_right_ref, rtaps_ref)
+    field = full_field(inside_ref, from_left_ref, from_right_ref, rtaps_ref)
     field_ref[...] = field
     copy = pltpu.make_async_copy(field_ref, field_hbm, sem)
     copy.start()
@@ -417,16 +431,18 @@
     edge = (3 * CY // 4, BLK)
     along, density, to_left, to_right = call(first_kernel, [(3 * CY, CX), (3 * CY, CX), edge, edge], 2)(recv, ltaps)
     from_left, from_right = exchanged(to_left, to_right)
+    (inside,) = call(inside_kernel, [(3 * CY, CX)], 2)(along, rtaps)
     edge = (CY // 4, BLK)
     dose, along, density, to_left, to_right = call(
         second_kernel, [(N_ROW, CAP), (CY, CX), (CY, CX), edge, edge], 7, (pltpu.VMEM((NT - 2, XR, SLOTS), BF),)
-    )(recv, along, density, from_left, from_right, rtaps, ltaps2)
+    )(recv, inside, density, from_left, from_right, rtaps, ltaps2)
     from_left, from_right = exchanged(to_left, to_right)
+    (inside,) = call(inside_kernel, [(CY, CX)], 2)(along, rtaps)
     field, final = call(
         third_kernel, [(CY, CX), (N_ROW, 1, CAP)], 7, (pltpu.VMEM((CY, CX), F32), pltpu.SemaphoreType.DMA),
         out_spaces=[pltpu.HBM, pltpu.VMEM],
     )(
-        recv, dose, along, density, from_left, from_right, rtaps
+        recv, dose, inside, density, from_left, from_right, rtaps
     )
     back = lax.all_to_all(final, "row", split_axis=0, concat_axis=0, tiled=True)
     (out,) = call(unpack_kernel, [(1, S_DEV)], 3)(back, owner, rank)

time: 56.1 us -> 55.7 us (level)
  waiting for transfers between devices: 8.09 us -> 7.49 us
    ppermute x2, waiting for transfers between devices: 1.48 us -> 0.89 us  [exchanged(): lax.ppermute(to_right, 'col', [(i, (i + 1) % n) for i in range(n)])]
    pallas_call x0 -> x2, Pallas kernels: none -> 0.58 us  [the longest x1 0.36 us: per_device(): inside, = call(inside_kernel, [(3 * CY, CX)], 2)(along, rtaps)]
  transfers between devices with their start and end apart: 4 -> 4, of which waited for: 4 -> 4; matrix products, arithmetic and copies ran while one was open for 0% -> 0% of each run, Pallas kernels for 0% -> 1%
where the time goes in v5:
time: 55.7 us; the launch traced here: 55.5 us
  blocking collectives  32.4 us (58%)
  Pallas kernels  11.8 us (21%)
  waiting for transfers between devices  7.49 us (13%)
  starting transfers between devices  3.07 us (6%)
  between operations  0.68 us (1%)
    all_to_all x1, blocking collectives, per_device(): recv = lax.all_to_all(send, 'row', split_axis=0, concat_axis=0, tiled=True)  20.8 us
    all_to_all x1, blocking collectives, per_device(): back = lax.all_to_all(final, 'row', split_axis=0, concat_axis=0, tiled=True)  11.7 us
    ppermute x2, waiting for transfers between devices, exchanged(): lax.ppermute(to_left, 'col', [((i + 1) % n, i) for i in range(n)])  6.61 us
    pallas_call x1, Pallas kernels, per_device(): call(second_kernel, [(N_ROW, CAP), (CY, CX), (CY, CX), edge, edge], 7, (p...  4.27 us
    pallas_call x1, Pallas kernels, per_device(): call(first_kernel, [(3 * CY, CX), (3 * CY, CX), edge, edge], 2)(recv, ltaps)  3.56 us
    ppermute x2, starting transfers between devices, exchanged(): lax.ppermute(to_right, 'col', [(i, (i + 1) % n) for i in range(n)])  2.58 us
    pallas_call x1, Pallas kernels, per_device(): call(pack_kernel, [(N_ROW, 1, 2 * NT * CAP), row, row], 4, rows, pltpu.HBM)  1.54 us
  transfers between devices with their start and end apart: 4, of which 4 were waited for; matrix products, arithmetic and copies ran while one was open for 0% of the time, Pallas kernels for 1%

profile of v5, /device:TPU:7, one launch (start us, length us, event | category | flops | bytes accessed | tf_op | source)
XLA Modules:
  0.0 55.5 jit_solution(5581479185853196217)
XLA Ops:
  0.6 1.5 %shard_map.86 = (f32[32,1,1280]{2,1,0:T(1,128)S(1)}, f32[1,2048]{1,0:T(1,128)S(1)}, f32[1,2048]{1,0:T(1,128)S(1)}) custom-call(f32[1,2048]{1,0:T(1,128)} %bitcast.6, s32[1,2048]{1,0:T(1,128)} %bitcast.7, s32[1,2048]{1,0:T(1,128)} %bitcast.8, s32[1,2048]{1,0:T(1,128)} %bitcast.9), custom_call_target="tpu_custom_call" | custom-call | tf_op jit(solution)/shard_map/pallas_call | solution.py:427
  2.2 0.0 copy-start.1
  2.2 20.8 %all_to_all.10.recv_ref = f32[32,1,1280]{2,1,0:T(1,128)S(1)} all-to-all(f32[32,1,1280]{2,1,0:T(1,128)S(1)} %get-tuple-element.16), channel_id=1, replica_groups=mesh['row'=32,'col'=8] {'row'}, dimensions={0} | all-to-all | bytes 327680 | tf_op jit(solution)/shard_map/all_to_all | solution.py:430
  22.9 0.0 copy-done.1
  22.9 0.0 copy-start
  23.0 3.6 %shard_map.87 = (f32[96,512]{1,0:T(8,128)S(1)}, f32[96,512]{1,0:T(8,128)S(1)}, f32[24,128]{1,0:T(8,128)S(1)}, f32[24,128]{1,0:T(8,128)S(1)}) custom-call(f32[32,1,1280]{2,1,0:T(1,128)S(1)} %all_to_all.10.recv_ref, bf16[192,320]{1,0:T(8,128)(2,1)S(1)} %copy-done.1), custom_call_target="tpu_custom_call" | custom-call | tf_op jit(solution)/shard_map/pallas_call | solution.py:432
  26.5 2.5 %collective-permute-start = (f32[24,128]{1,0:T(8,128)S(1)}, f32[24,128]{1,0:T(8,128)S(1)}, u32[]{:S(2)}, u32[]{:S(2)}) collective-permute-start(f32[24,128]{1,0:T(8,128)S(1)} %get-tuple-element.19), channel_id=1, source_target_pairs={{0,1},{1,2},{2,3},{3,4},{4,5},{5,6},{6,7},{7,0},{8,9},{9,10},{10,1... | collective-permute-start | bytes 36872 | tf_op jit(solution)/shard_map/ppermute | solution.py:416
  29.1 0.0 collective-permute-start.1
  29.1 0.0 copy-done
  29.1 0.0 copy-start.2
  29.1 0.4 shard_map.88.inside_ref
  29.4 0.5 collective-permute-done.from_left_ref
  29.9 3.5 %collective-permute-done.1.from_right_ref = f32[24,128]{1,0:T(8,128)S(1)} collective-permute-done((f32[24,128]{1,0:T(8,128)S(1)}, f32[24,128]{1,0:T(8,128)S(1)}, u32[]{:S(2)}, u32[]{:S(2)}) %collective-permute-start.1) | collective-permute-done | bytes 12320 | tf_op jit(solution)/shard_map/ppermute | solution.py:417
  33.4 0.0 copy-done.2
  33.4 4.3 %shard_map.89 = (f32[32,128]{1,0:T(8,128)S(1)}, f32[32,512]{1,0:T(8,128)S(1)}, f32[32,512]{1,0:T(8,128)S(1)}, f32[8,128]{1,0:T(8,128)S(1)}, f32[8,128]{1,0:T(8,128)S(1)}) custom-call(f32[32,1,1280]{2,1,0:T(1,128)S(1)} %all_to_all.10.recv_ref, f32[96,512]{1,0:T(8,128)S(1)} %shard_map.88.inside_ref, f32[96,512]{1,0:T(8,128)S(1)} %get-tuple-element.18.density_ref, ...), custom_call_target="tpu_custom_call" | custom-call | tf_op jit(solution)/shard_map/pallas_call | solution.py:436
  37.7 0.1 collective-permute-start.2
  37.7 0.5 collective-permute-start.3
  38.2 0.2 shard_map.90.inside_ref
  38.4 0.4 collective-permute-done.2.from_left_ref
  38.8 3.1 %collective-permute-done.3.from_right_ref = f32[8,128]{1,0:T(8,128)S(1)} collective-permute-done((f32[8,128]{1,0:T(8,128)S(1)}, f32[8,128]{1,0:T(8,128)S(1)}, u32[]{:S(2)}, u32[]{:S(2)}) %collective-permute-start.3) | collective-permute-done | bytes 4128 | tf_op jit(solution)/shard_map/ppermute | solution.py:417
  41.9 1.0 %shard_map.91 = (f32[32,512]{1,0:T(8,128)}, f32[32,1,128]{2,1,0:T(1,128)S(1)}) custom-call(f32[32,1,1280]{2,1,0:T(1,128)S(1)} %all_to_all.10.recv_ref, f32[32,128]{1,0:T(8,128)S(1)} %get-tuple-element.21.dose_ref, f32[32,512]{1,0:T(8,128)S(1)} %shard_map.90.inside_ref, f32[32,512]{1,0:T(8,128)S(1)} %get-tuple-element.23.density_ref, ...), custom_call_target="tpu_custom_call" | custom-call | tf_op jit(solution)/shard_map/pallas_call | solution.py:441
  42.9 11.7 %all_to_all.11.ret_ref = f32[32,1,128]{2,1,0:T(1,128)S(1)} all-to-all(f32[32,1,128]{2,1,0:T(1,128)S(1)} %get-tuple-element.26), channel_id=1, replica_groups=mesh['row'=32,'col'=8] {'row'}, dimensions={0} | all-to-all | bytes 32768 | tf_op jit(solution)/shard_map/all_to_all | solution.py:447
  54.6 0.9 %shard_map.92 = f32[1,2048]{1,0:T(1,128)} custom-call(f32[32,1,128]{2,1,0:T(1,128)S(1)} %all_to_all.11.ret_ref, f32[1,2048]{1,0:T(1,128)S(1)} %get-tuple-element.27.owner_ref, f32[1,2048]{1,0:T(1,128)S(1)} %get-tuple-element.28.rank_ref), custom_call_target="tpu_custom_call" | custom-call | tf_op jit(solution)/shard_map/pallas_call | solution.py:448
Async XLA Ops:
  2.2 20.8 %copy-start.1 = (bf16[192,320]{1,0:T(8,128)(2,1)S(1)}, bf16[192,320]{1,0:T(8,128)(2,1)}, u32[]{:S(2)}) copy-start(bf16[192,320]{1,0:T(8,128)(2,1)} %constant.6.clone.ltaps_ref) | copy-start | bytes 368644
  22.9 6.1 %copy-start = (bf16[384,256]{1,0:T(8,128)(2,1)S(1)}, bf16[384,256]{1,0:T(8,128)(2,1)}, u32[]{:S(2)}) copy-start(bf16[384,256]{1,0:T(8,128)(2,1)} %constant.8.clone.rtaps_ref) | copy-start | bytes 589828
  26.5 3.4 %collective-permute-start = (f32[24,128]{1,0:T(8,128)S(1)}, f32[24,128]{1,0:T(8,128)S(1)}, u32[]{:S(2)}, u32[]{:S(2)}) collective-permute-start(f32[24,128]{1,0:T(8,128)S(1)} %get-tuple-element.19), channel_id=1, source_target_pairs={{0,1},{1,2},{2,3},{3,4},{4,5},{5,6},{6,7},{7,0},{8,9},{9,10},{10,1... | collective-permute-start | bytes 36872 | tf_op jit(solution)/shard_map/ppermute | solution.py:416
  29.1 4.3 %collective-permute-start.1 = (f32[24,128]{1,0:T(8,128)S(1)}, f32[24,128]{1,0:T(8,128)S(1)}, u32[]{:S(2)}, u32[]{:S(2)}) collective-permute-start(f32[24,128]{1,0:T(8,128)S(1)} %get-tuple-element.20), channel_id=1, source_target_pairs={{1,0},{2,1},{3,2},{4,3},{5,4},{6,5},{7,6},{0,7},{9,8},{10,9},{11,1... | collective-permute-start | bytes 36872 | tf_op jit(solution)/shard_map/ppermute | solution.py:417
  29.1 4.3 %copy-start.2 = (bf16[64,192]{1,0:T(8,128)(2,1)S(1)}, bf16[64,192]{1,0:T(8,128)(2,1)}, u32[]{:S(2)}) copy-start(bf16[64,192]{1,0:T(8,128)(2,1)} %constant.7.clone.ltaps_ref) | copy-start | bytes 73732
  37.7 1.2 %collective-permute-start.2 = (f32[8,128]{1,0:T(8,128)S(1)}, f32[8,128]{1,0:T(8,128)S(1)}, u32[]{:S(2)}, u32[]{:S(2)}) collective-permute-start(f32[8,128]{1,0:T(8,128)S(1)} %get-tuple-element.24), channel_id=1, source_target_pairs={{0,1},{1,2},{2,3},{3,4},{4,5},{5,6},{6,7},{7,0},{8,9},{9,10},{10,1... | collective-permute-start | bytes 12296 | tf_op jit(solution)/shard_map/ppermute | solution.py:416
  37.7 4.2 %collective-permute-start.3 = (f32[8,128]{1,0:T(8,128)S(1)}, f32[8,128]{1,0:T(8,128)S(1)}, u32[]{:S(2)}, u32[]{:S(2)}) collective-permute-start(f32[8,128]{1,0:T(8,128)S(1)} %get-tuple-element.25), channel_id=1, source_target_pairs={{1,0},{2,1},{3,2},{4,3},{5,4},{6,5},{7,6},{0,7},{9,8},{10,9},{11,1... | collective-permute-start | bytes 12296 | tf_op jit(solution)/shard_map/ppermute | solution.py:417

commit v6 on v5

--- a/solution.py
+++ b/solution.py
@@ -48,7 +48,8 @@
 
 def left_constant(rows, cols, offset):
     hi, lo = two(band(rows, cols, offset))
-    return np.concatenate([np.concatenate([hi, hi], 1), np.concatenate([lo, lo], 1)], 0)
+    tiles = [slice(n, n + CY) for n in range(0, cols, CY)]
+    return np.stack([np.concatenate([np.concatenate([m[:, n], m[:, n]], 1) for m in (hi, lo)], 0) for n in tiles])
 
 
 def right_constant():
@@ -121,8 +122,8 @@
     ones = chosen(mine, jnp.ones((1, S_DEV), F32))
     stacked = jnp.concatenate([ones[:, c * chunk:(c + 1) * chunk] for c in range(n_chunks)], 0)
     prefix = nn_dot(stacked, before)
-    totals = nn_dot(stacked, jnp.ones((chunk, chunk), BF))
-    base = jnp.zeros((N_ROW, chunk), F32)
+    totals = prefix[:, chunk - 1:] + stacked[:, chunk - 1:].astype(F32)
+    base = jnp.zeros((N_ROW, 1), F32)
     ranks = []
     for c in range(n_chunks):
         here = slice(c * N_ROW, (c + 1) * N_ROW)
@@ -173,8 +174,8 @@
 
 
 def column_chunk(shot, i):
-    first, second = over_rows(shot["column"], i), over_rows(shot["column1"], i)
-    w0, w1 = over_rows(shot["x0"], i), over_rows(shot["x1"], i)
+    first, w1 = over_rows(shot["column"], i), over_rows(shot["x1"], i)
+    second, w0 = first + jnp.ones_like(first), jnp.ones_like(w1) - w1
     none = jnp.zeros_like(w0)
     out = []
     for k in range(XR // SUB16):
@@ -184,7 +185,8 @@
 
 
 def row_chunk(shot, dosed, i, at_dosed):
-    first, second = over_rows(shot["y"], i), over_rows(shot["y1"], i)
+    first = over_rows(shot["y"], i)
+    second = first + jnp.ones_like(first)
     block = over_rows(shot["block"], i)
     values = [over_rows(v, at_dosed) for v in dosed]
     none = jnp.zeros_like(first)
@@ -252,9 +254,10 @@
     return jnp.concatenate(parts, 0)
 
 
-def blurred_y(density, taps_ref):
-    hi, lo = split2(density)
-    both = nn_dot(taps_ref[...], jnp.concatenate([hi, lo], 0))
+def blurred_y(tiles, taps_ref):
+    both = None
+    for n, density in enumerate(tiles):
+        both = added(both, nn_dot(taps_ref[n], jnp.concatenate(split2(density), 0)))
     rows = both.shape[0] // 2
     return both[:rows] + both[rows:]
 
@@ -300,7 +303,8 @@
     for j in range(2):
         here = slice(j * CAP, (j + 1) * CAP)
         g = both[:BLK, here] + both[BLK:, here]
-        block, y, y1, w0, w1 = (shot[name][i + j:i + j + 1] for name in ("block", "y", "y1", "y0w", "y1w"))
+        block, y, w1 = (jnp.broadcast_to(shot[name][i + j:i + j + 1], (8, CAP)) for name in ("block", "y", "y1w"))
+        block, y, w1, y1, w0 = (jnp.concatenate([v] * (CY // 8), 0) for v in (block, y, w1, y + 1.0, 1.0 - w1))
         mine = g[:CY]
         for h in range(1, NB):
             mine = jnp.where(block == float(h), g[h * CY:(h + 1) * CY], mine)
@@ -325,7 +329,7 @@
         shot = decoded(place)
         tiles.append(tile_density(shot, dose))
     density_ref[...] = jnp.concatenate(tiles[1:NT - 1], 0)
-    along = blurred_y(jnp.concatenate(tiles, 0), ltaps_ref)
+    along = blurred_y(tiles, ltaps_ref)
     along_ref[...] = along
     to_left_ref[...] = packed_edge(along[:, :BLK], 0)
     to_right_ref[...] = packed_edge(along[:, CX - BLK:], BLK - 32)
@@ -370,7 +374,7 @@
             dosed = dosed_weights(shots[n], dose, sources)
     tiles = [assembled(both) for both in densities]
     density2_ref[...] = tiles[1]
-    along = blurred_y(jnp.concatenate(tiles, 0), ltaps_ref)
+    along = blurred_y(tiles, ltaps_ref)
     along2_ref[...] = along
     to_left_ref[...] = packed_edge(along[:, :BLK], 0)
     to_right_ref[...] = packed_edge(along[:, CX - BLK:], BLK - 32)

time: 55.7 us -> 55.5 us (level)
  no operation moved by 1% of the time
where the time goes in v6:
time: 55.5 us; the launch traced here: 55.4 us
  blocking collectives  32.3 us (58%)
  Pallas kernels  11.8 us (21%)
  waiting for transfers between devices  7.49 us (13%)
  starting transfers between devices  3.07 us (6%)
  between operations  0.68 us (1%)
    all_to_all x1, blocking collectives, per_device(): recv = lax.all_to_all(send, 'row', split_axis=0, concat_axis=0, tiled=True)  20.6 us
    all_to_all x1, blocking collectives, per_device(): back = lax.all_to_all(final, 'row', split_axis=0, concat_axis=0, tiled=True)  11.7 us
    ppermute x2, waiting for transfers between devices, exchanged(): lax.ppermute(to_left, 'col', [((i + 1) % n, i) for i in range(n)])  6.61 us
    pallas_call x1, Pallas kernels, per_device(): call(second_kernel, [(N_ROW, CAP), (CY, CX), (CY, CX), edge, edge], 7, (p...  4.31 us
    pallas_call x1, Pallas kernels, per_device(): call(first_kernel, [(3 * CY, CX), (3 * CY, CX), edge, edge], 2)(recv, ltaps)  3.51 us
    ppermute x2, starting transfers between devices, exchanged(): lax.ppermute(to_right, 'col', [(i, (i + 1) % n) for i in range(n)])  2.58 us
    pallas_call x1, Pallas kernels, per_device(): call(pack_kernel, [(N_ROW, 1, 2 * NT * CAP), row, row], 4, rows, pltpu.HBM)  1.57 us
  transfers between devices with their start and end apart: 4, of which 4 were waited for; matrix products, arithmetic and copies ran while one was open for 0% of the time, Pallas kernels for 1%

profile of v6, /device:TPU:7, one launch (start us, length us, event | category | flops | bytes accessed | tf_op | source)
XLA Modules:
  0.0 55.4 jit_solution(5520933568454003121)
XLA Ops:
  0.6 0.0 copy-start.1
  0.6 1.6 %shard_map.86 = (f32[32,1,1280]{2,1,0:T(1,128)S(1)}, f32[1,2048]{1,0:T(1,128)S(1)}, f32[1,2048]{1,0:T(1,128)S(1)}) custom-call(f32[1,2048]{1,0:T(1,128)} %bitcast.6, s32[1,2048]{1,0:T(1,128)} %bitcast.7, s32[1,2048]{1,0:T(1,128)} %bitcast.8, s32[1,2048]{1,0:T(1,128)} %bitcast.9), custom_call_target="tpu_custom_call" | custom-call | tf_op jit(solution)/shard_map/pallas_call | solution.py:431
  2.2 20.6 %all_to_all.10.recv_ref = f32[32,1,1280]{2,1,0:T(1,128)S(1)} all-to-all(f32[32,1,1280]{2,1,0:T(1,128)S(1)} %get-tuple-element.16), channel_id=1, replica_groups=mesh['row'=32,'col'=8] {'row'}, dimensions={0} | all-to-all | bytes 327680 | tf_op jit(solution)/shard_map/all_to_all | solution.py:434
  22.8 0.0 copy-done.1
  22.8 0.0 copy-start
  22.8 3.5 %shard_map.87 = (f32[96,512]{1,0:T(8,128)S(1)}, f32[96,512]{1,0:T(8,128)S(1)}, f32[24,128]{1,0:T(8,128)S(1)}, f32[24,128]{1,0:T(8,128)S(1)}) custom-call(f32[32,1,1280]{2,1,0:T(1,128)S(1)} %all_to_all.10.recv_ref, bf16[5,192,64]{2,1,0:T(8,128)(2,1)S(1)} %copy-done.1), custom_call_target="tpu_custom_call" | custom-call | tf_op jit(solution)/shard_map/pallas_call | solution.py:436
  26.4 2.5 %collective-permute-start = (f32[24,128]{1,0:T(8,128)S(1)}, f32[24,128]{1,0:T(8,128)S(1)}, u32[]{:S(2)}, u32[]{:S(2)}) collective-permute-start(f32[24,128]{1,0:T(8,128)S(1)} %get-tuple-element.19), channel_id=1, source_target_pairs={{0,1},{1,2},{2,3},{3,4},{4,5},{5,6},{6,7},{7,0},{8,9},{9,10},{10,1... | collective-permute-start | bytes 36872 | tf_op jit(solution)/shard_map/ppermute | solution.py:420
  28.9 0.0 collective-permute-start.1
  28.9 0.0 copy-done
  28.9 0.0 copy-start.2
  28.9 0.4 shard_map.88.inside_ref
  29.3 0.5 collective-permute-done.from_left_ref
  29.7 3.5 %collective-permute-done.1.from_right_ref = f32[24,128]{1,0:T(8,128)S(1)} collective-permute-done((f32[24,128]{1,0:T(8,128)S(1)}, f32[24,128]{1,0:T(8,128)S(1)}, u32[]{:S(2)}, u32[]{:S(2)}) %collective-permute-start.1) | collective-permute-done | bytes 12320 | tf_op jit(solution)/shard_map/ppermute | solution.py:421
  33.2 0.0 copy-done.2
  33.2 4.3 %shard_map.89 = (f32[32,128]{1,0:T(8,128)S(1)}, f32[32,512]{1,0:T(8,128)S(1)}, f32[32,512]{1,0:T(8,128)S(1)}, f32[8,128]{1,0:T(8,128)S(1)}, f32[8,128]{1,0:T(8,128)S(1)}) custom-call(f32[32,1,1280]{2,1,0:T(1,128)S(1)} %all_to_all.10.recv_ref, f32[96,512]{1,0:T(8,128)S(1)} %shard_map.88.inside_ref, f32[96,512]{1,0:T(8,128)S(1)} %get-tuple-element.18.density_ref, ...), custom_call_target="tpu_custom_call" | custom-call | tf_op jit(solution)/shard_map/pallas_call | solution.py:440
  37.5 0.0 collective-permute-start.2
  37.6 0.5 collective-permute-start.3
  38.1 0.2 shard_map.90.inside_ref
  38.3 0.4 collective-permute-done.2.from_left_ref
  38.7 3.1 %collective-permute-done.3.from_right_ref = f32[8,128]{1,0:T(8,128)S(1)} collective-permute-done((f32[8,128]{1,0:T(8,128)S(1)}, f32[8,128]{1,0:T(8,128)S(1)}, u32[]{:S(2)}, u32[]{:S(2)}) %collective-permute-start.3) | collective-permute-done | bytes 4128 | tf_op jit(solution)/shard_map/ppermute | solution.py:421
  41.8 0.9 %shard_map.91 = (f32[32,512]{1,0:T(8,128)}, f32[32,1,128]{2,1,0:T(1,128)S(1)}) custom-call(f32[32,1,1280]{2,1,0:T(1,128)S(1)} %all_to_all.10.recv_ref, f32[32,128]{1,0:T(8,128)S(1)} %get-tuple-element.21.dose_ref, f32[32,512]{1,0:T(8,128)S(1)} %shard_map.90.inside_ref, f32[32,512]{1,0:T(8,128)S(1)} %get-tuple-element.23.density_ref, ...), custom_call_target="tpu_custom_call" | custom-call | tf_op jit(solution)/shard_map/pallas_call | solution.py:445
  42.8 11.7 %all_to_all.11.ret_ref = f32[32,1,128]{2,1,0:T(1,128)S(1)} all-to-all(f32[32,1,128]{2,1,0:T(1,128)S(1)} %get-tuple-element.26), channel_id=1, replica_groups=mesh['row'=32,'col'=8] {'row'}, dimensions={0} | all-to-all | bytes 32768 | tf_op jit(solution)/shard_map/all_to_all | solution.py:451
  54.5 0.9 %shard_map.92 = f32[1,2048]{1,0:T(1,128)} custom-call(f32[32,1,128]{2,1,0:T(1,128)S(1)} %all_to_all.11.ret_ref, f32[1,2048]{1,0:T(1,128)S(1)} %get-tuple-element.27.owner_ref, f32[1,2048]{1,0:T(1,128)S(1)} %get-tuple-element.28.rank_ref), custom_call_target="tpu_custom_call" | custom-call | tf_op jit(solution)/shard_map/pallas_call | solution.py:452
Async XLA Ops:
  0.6 22.2 %copy-start.1 = (bf16[5,192,64]{2,1,0:T(8,128)(2,1)S(1)}, bf16[5,192,64]{2,1,0:T(8,128)(2,1)}, u32[]{:S(2)}) copy-start(bf16[5,192,64]{2,1,0:T(8,128)(2,1)} %constant.6.clone.ltaps_ref) | copy-start | bytes 368644
  22.8 6.1 %copy-start = (bf16[384,256]{1,0:T(8,128)(2,1)S(1)}, bf16[384,256]{1,0:T(8,128)(2,1)}, u32[]{:S(2)}) copy-start(bf16[384,256]{1,0:T(8,128)(2,1)} %constant.8.clone.rtaps_ref) | copy-start | bytes 589828
  26.4 3.4 %collective-permute-start = (f32[24,128]{1,0:T(8,128)S(1)}, f32[24,128]{1,0:T(8,128)S(1)}, u32[]{:S(2)}, u32[]{:S(2)}) collective-permute-start(f32[24,128]{1,0:T(8,128)S(1)} %get-tuple-element.19), channel_id=1, source_target_pairs={{0,1},{1,2},{2,3},{3,4},{4,5},{5,6},{6,7},{7,0},{8,9},{9,10},{10,1... | collective-permute-start | bytes 36872 | tf_op jit(solution)/shard_map/ppermute | solution.py:420
  28.9 4.3 %collective-permute-start.1 = (f32[24,128]{1,0:T(8,128)S(1)}, f32[24,128]{1,0:T(8,128)S(1)}, u32[]{:S(2)}, u32[]{:S(2)}) collective-permute-start(f32[24,128]{1,0:T(8,128)S(1)} %get-tuple-element.20), channel_id=1, source_target_pairs={{1,0},{2,1},{3,2},{4,3},{5,4},{6,5},{7,6},{0,7},{9,8},{10,9},{11,1... | collective-permute-start | bytes 36872 | tf_op jit(solution)/shard_map/ppermute | solution.py:421
  28.9 4.3 %copy-start.2 = (bf16[3,64,64]{2,1,0:T(8,128)(2,1)S(1)}, bf16[3,64,64]{2,1,0:T(8,128)(2,1)}, u32[]{:S(2)}) copy-start(bf16[3,64,64]{2,1,0:T(8,128)(2,1)} %constant.7.clone.ltaps_ref) | copy-start | bytes 73732
  37.5 1.2 %collective-permute-start.2 = (f32[8,128]{1,0:T(8,128)S(1)}, f32[8,128]{1,0:T(8,128)S(1)}, u32[]{:S(2)}, u32[]{:S(2)}) collective-permute-start(f32[8,128]{1,0:T(8,128)S(1)} %get-tuple-element.24), channel_id=1, source_target_pairs={{0,1},{1,2},{2,3},{3,4},{4,5},{5,6},{6,7},{7,0},{8,9},{9,10},{10,1... | collective-permute-start | bytes 12296 | tf_op jit(solution)/shard_map/ppermute | solution.py:420
  37.6 4.2 %collective-permute-start.3 = (f32[8,128]{1,0:T(8,128)S(1)}, f32[8,128]{1,0:T(8,128)S(1)}, u32[]{:S(2)}, u32[]{:S(2)}) collective-permute-start(f32[8,128]{1,0:T(8,128)S(1)} %get-tuple-element.25), channel_id=1, source_target_pairs={{1,0},{2,1},{3,2},{4,3},{5,4},{6,5},{7,6},{0,7},{9,8},{10,9},{11,1... | collective-permute-start | bytes 12296 | tf_op jit(solution)/shard_map/ppermute | solution.py:421

commit v7 on v6

--- a/solution.py
+++ b/solution.py
@@ -303,8 +303,7 @@
     for j in range(2):
         here = slice(j * CAP, (j + 1) * CAP)
         g = both[:BLK, here] + both[BLK:, here]
-        block, y, w1 = (jnp.broadcast_to(shot[name][i + j:i + j + 1], (8, CAP)) for name in ("block", "y", "y1w"))
-        block, y, w1, y1, w0 = (jnp.concatenate([v] * (CY // 8), 0) for v in (block, y, w1, y + 1.0, 1.0 - w1))
+        block, y, y1, w0, w1 = (shot[name][i + j:i + j + 1] for name in ("block", "y", "y1", "y0w", "y1w"))
         mine = g[:CY]
         for h in range(1, NB):
             mine = jnp.where(block == float(h), g[h * CY:(h + 1) * CY], mine)

time: 55.5 us -> 55.5 us (level)
  no operation moved by 1% of the time
where the time goes in v7:
time: 55.5 us; the launch traced here: 55.4 us
  blocking collectives  32.3 us (58%)
  Pallas kernels  11.8 us (21%)
  waiting for transfers between devices  7.5 us (14%)
  starting transfers between devices  3.07 us (6%)
  between operations  0.68 us (1%)
    all_to_all x1, blocking collectives, per_device(): recv = lax.all_to_all(send, 'row', split_axis=0, concat_axis=0, tiled=True)  20.6 us
    all_to_all x1, blocking collectives, per_device(): back = lax.all_to_all(final, 'row', split_axis=0, concat_axis=0, tiled=True)  11.7 us
    ppermute x2, waiting for transfers between devices, exchanged(): lax.ppermute(to_left, 'col', [((i + 1) % n, i) for i in range(n)])  6.61 us
    pallas_call x1, Pallas kernels, per_device(): call(second_kernel, [(N_ROW, CAP), (CY, CX), (CY, CX), edge, edge], 7, (p...  4.29 us
    pallas_call x1, Pallas kernels, per_device(): call(first_kernel, [(3 * CY, CX), (3 * CY, CX), edge, edge], 2)(recv, ltaps)  3.51 us
    ppermute x2, starting transfers between devices, exchanged(): lax.ppermute(to_right, 'col', [(i, (i + 1) % n) for i in range(n)])  2.58 us
    pallas_call x1, Pallas kernels, per_device(): call(pack_kernel, [(N_ROW, 1, 2 * NT * CAP), row, row], 4, rows, pltpu.HBM)  1.57 us
  transfers between devices with their start and end apart: 4, of which 4 were waited for; matrix products, arithmetic and copies ran while one was open for 0% of the time, Pallas kernels for 1%

profile of v7, /device:TPU:7, one launch (start us, length us, event | category | flops | bytes accessed | tf_op | source)
XLA Modules:
  0.0 55.4 jit_solution(14461703930355758858)
XLA Ops:
  0.6 0.0 copy-start.1
  0.6 1.6 %shard_map.86 = (f32[32,1,1280]{2,1,0:T(1,128)S(1)}, f32[1,2048]{1,0:T(1,128)S(1)}, f32[1,2048]{1,0:T(1,128)S(1)}) custom-call(f32[1,2048]{1,0:T(1,128)} %bitcast.6, s32[1,2048]{1,0:T(1,128)} %bitcast.7, s32[1,2048]{1,0:T(1,128)} %bitcast.8, s32[1,2048]{1,0:T(1,128)} %bitcast.9), custom_call_target="tpu_custom_call" | custom-call | tf_op jit(solution)/shard_map/pallas_call | solution.py:430
  2.2 20.6 %all_to_all.10.recv_ref = f32[32,1,1280]{2,1,0:T(1,128)S(1)} all-to-all(f32[32,1,1280]{2,1,0:T(1,128)S(1)} %get-tuple-element.16), channel_id=1, replica_groups=mesh['row'=32,'col'=8] {'row'}, dimensions={0} | all-to-all | bytes 327680 | tf_op jit(solution)/shard_map/all_to_all | solution.py:433
  22.8 0.0 copy-done.1
  22.8 0.0 copy-start
  22.8 3.5 %shard_map.87 = (f32[96,512]{1,0:T(8,128)S(1)}, f32[96,512]{1,0:T(8,128)S(1)}, f32[24,128]{1,0:T(8,128)S(1)}, f32[24,128]{1,0:T(8,128)S(1)}) custom-call(f32[32,1,1280]{2,1,0:T(1,128)S(1)} %all_to_all.10.recv_ref, bf16[5,192,64]{2,1,0:T(8,128)(2,1)S(1)} %copy-done.1), custom_call_target="tpu_custom_call" | custom-call | tf_op jit(solution)/shard_map/pallas_call | solution.py:435
  26.4 2.5 %collective-permute-start = (f32[24,128]{1,0:T(8,128)S(1)}, f32[24,128]{1,0:T(8,128)S(1)}, u32[]{:S(2)}, u32[]{:S(2)}) collective-permute-start(f32[24,128]{1,0:T(8,128)S(1)} %get-tuple-element.19), channel_id=1, source_target_pairs={{0,1},{1,2},{2,3},{3,4},{4,5},{5,6},{6,7},{7,0},{8,9},{9,10},{10,1... | collective-permute-start | bytes 36872 | tf_op jit(solution)/shard_map/ppermute | solution.py:419
  28.9 0.0 collective-permute-start.1
  28.9 0.0 copy-done
  28.9 0.0 copy-start.2
  28.9 0.4 shard_map.88.inside_ref
  29.3 0.5 collective-permute-done.from_left_ref
  29.7 3.5 %collective-permute-done.1.from_right_ref = f32[24,128]{1,0:T(8,128)S(1)} collective-permute-done((f32[24,128]{1,0:T(8,128)S(1)}, f32[24,128]{1,0:T(8,128)S(1)}, u32[]{:S(2)}, u32[]{:S(2)}) %collective-permute-start.1) | collective-permute-done | bytes 12320 | tf_op jit(solution)/shard_map/ppermute | solution.py:420
  33.2 0.0 copy-done.2
  33.2 4.3 %shard_map.89 = (f32[32,128]{1,0:T(8,128)S(1)}, f32[32,512]{1,0:T(8,128)S(1)}, f32[32,512]{1,0:T(8,128)S(1)}, f32[8,128]{1,0:T(8,128)S(1)}, f32[8,128]{1,0:T(8,128)S(1)}) custom-call(f32[32,1,1280]{2,1,0:T(1,128)S(1)} %all_to_all.10.recv_ref, f32[96,512]{1,0:T(8,128)S(1)} %shard_map.88.inside_ref, f32[96,512]{1,0:T(8,128)S(1)} %get-tuple-element.18.density_ref, ...), custom_call_target="tpu_custom_call" | custom-call | tf_op jit(solution)/shard_map/pallas_call | solution.py:439
  37.5 0.1 collective-permute-start.2
  37.6 0.5 collective-permute-start.3
  38.0 0.2 shard_map.90.inside_ref
  38.3 0.4 collective-permute-done.2.from_left_ref
  38.7 3.1 %collective-permute-done.3.from_right_ref = f32[8,128]{1,0:T(8,128)S(1)} collective-permute-done((f32[8,128]{1,0:T(8,128)S(1)}, f32[8,128]{1,0:T(8,128)S(1)}, u32[]{:S(2)}, u32[]{:S(2)}) %collective-permute-start.3) | collective-permute-done | bytes 4128 | tf_op jit(solution)/shard_map/ppermute | solution.py:420
  41.8 1.0 %shard_map.91 = (f32[32,512]{1,0:T(8,128)}, f32[32,1,128]{2,1,0:T(1,128)S(1)}) custom-call(f32[32,1,1280]{2,1,0:T(1,128)S(1)} %all_to_all.10.recv_ref, f32[32,128]{1,0:T(8,128)S(1)} %get-tuple-element.21.dose_ref, f32[32,512]{1,0:T(8,128)S(1)} %shard_map.90.inside_ref, f32[32,512]{1,0:T(8,128)S(1)} %get-tuple-element.23.density_ref, ...), custom_call_target="tpu_custom_call" | custom-call | tf_op jit(solution)/shard_map/pallas_call | solution.py:444
  42.8 11.7 %all_to_all.11.ret_ref = f32[32,1,128]{2,1,0:T(1,128)S(1)} all-to-all(f32[32,1,128]{2,1,0:T(1,128)S(1)} %get-tuple-element.26), channel_id=1, replica_groups=mesh['row'=32,'col'=8] {'row'}, dimensions={0} | all-to-all | bytes 32768 | tf_op jit(solution)/shard_map/all_to_all | solution.py:450
  54.5 0.9 %shard_map.92 = f32[1,2048]{1,0:T(1,128)} custom-call(f32[32,1,128]{2,1,0:T(1,128)S(1)} %all_to_all.11.ret_ref, f32[1,2048]{1,0:T(1,128)S(1)} %get-tuple-element.27.owner_ref, f32[1,2048]{1,0:T(1,128)S(1)} %get-tuple-element.28.rank_ref), custom_call_target="tpu_custom_call" | custom-call | tf_op jit(solution)/shard_map/pallas_call | solution.py:451
Async XLA Ops:
  0.6 22.2 %copy-start.1 = (bf16[5,192,64]{2,1,0:T(8,128)(2,1)S(1)}, bf16[5,192,64]{2,1,0:T(8,128)(2,1)}, u32[]{:S(2)}) copy-start(bf16[5,192,64]{2,1,0:T(8,128)(2,1)} %constant.6.clone.ltaps_ref) | copy-start | bytes 368644
  22.8 6.1 %copy-start = (bf16[384,256]{1,0:T(8,128)(2,1)S(1)}, bf16[384,256]{1,0:T(8,128)(2,1)}, u32[]{:S(2)}) copy-start(bf16[384,256]{1,0:T(8,128)(2,1)} %constant.8.clone.rtaps_ref) | copy-start | bytes 589828
  26.4 3.4 %collective-permute-start = (f32[24,128]{1,0:T(8,128)S(1)}, f32[24,128]{1,0:T(8,128)S(1)}, u32[]{:S(2)}, u32[]{:S(2)}) collective-permute-start(f32[24,128]{1,0:T(8,128)S(1)} %get-tuple-element.19), channel_id=1, source_target_pairs={{0,1},{1,2},{2,3},{3,4},{4,5},{5,6},{6,7},{7,0},{8,9},{9,10},{10,1... | collective-permute-start | bytes 36872 | tf_op jit(solution)/shard_map/ppermute | solution.py:419
  28.9 4.3 %collective-permute-start.1 = (f32[24,128]{1,0:T(8,128)S(1)}, f32[24,128]{1,0:T(8,128)S(1)}, u32[]{:S(2)}, u32[]{:S(2)}) collective-permute-start(f32[24,128]{1,0:T(8,128)S(1)} %get-tuple-element.20), channel_id=1, source_target_pairs={{1,0},{2,1},{3,2},{4,3},{5,4},{6,5},{7,6},{0,7},{9,8},{10,9},{11,1... | collective-permute-start | bytes 36872 | tf_op jit(solution)/shard_map/ppermute | solution.py:420
  28.9 4.3 %copy-start.2 = (bf16[3,64,64]{2,1,0:T(8,128)(2,1)S(1)}, bf16[3,64,64]{2,1,0:T(8,128)(2,1)}, u32[]{:S(2)}) copy-start(bf16[3,64,64]{2,1,0:T(8,128)(2,1)} %constant.7.clone.ltaps_ref) | copy-start | bytes 73732
  37.5 1.2 %collective-permute-start.2 = (f32[8,128]{1,0:T(8,128)S(1)}, f32[8,128]{1,0:T(8,128)S(1)}, u32[]{:S(2)}, u32[]{:S(2)}) collective-permute-start(f32[8,128]{1,0:T(8,128)S(1)} %get-tuple-element.24), channel_id=1, source_target_pairs={{0,1},{1,2},{2,3},{3,4},{4,5},{5,6},{6,7},{7,0},{8,9},{9,10},{10,1... | collective-permute-start | bytes 12296 | tf_op jit(solution)/shard_map/ppermute | solution.py:419
  37.6 4.2 %collective-permute-start.3 = (f32[8,128]{1,0:T(8,128)S(1)}, f32[8,128]{1,0:T(8,128)S(1)}, u32[]{:S(2)}, u32[]{:S(2)}) collective-permute-start(f32[8,128]{1,0:T(8,128)S(1)} %get-tuple-element.25), channel_id=1, source_target_pairs={{1,0},{2,1},{3,2},{4,3},{5,4},{6,5},{7,6},{0,7},{9,8},{10,9},{11,1... | collective-permute-start | bytes 12296 | tf_op jit(solution)/shard_map/ppermute | solution.py:420
